TPU v7x, 128 devices: a whole 4x4x4 slice. The times are simulated.
128 devices in a mesh: row: 8 (over z, y_lo), col: 16 (over y_hi, x, core).
Axes of the slice: x: 4, y: 4 (y_hi: 2, y_lo: 2; y = y_hi * 2 + y_lo), z: 4, core: 2. Of those that a mesh axis runs over, the one named last changes fastest.
Arguments:
- tiles: float32 [8, 16, 256, 128, 128], P('row', 'col'), may hold values from -0.125 to 0.125
- tile_rows: int32 [8, 16, 256], P('row', 'col'), may hold values from 0 to 255, as said below
- tile_cols: int32 [8, 16, 256], P('row', 'col'), may hold values from 0 to 127, as said below
- tile_counts: int32 [8, 16], P('row', 'col'), may hold values from 1 to 256, as said below
- block_now: float32 [8, 262144], P(None, ('row', 'col')), may hold values from -6 to 6
- block_prev: float32 [8, 262144], P(None, ('row', 'col')), may hold values from -6 to 6
- coupling: float32 [8, 8], replicated, may hold values from -3 to 3
- diag_energy: float32 [262144], P(('row', 'col')), may hold values from 1 to 4
Outputs:
- next_block: float32 [8, 262144], P(None, ('row', 'col'))
- alpha: float32 [8, 8], replicated
- beta: float32 [8, 8], replicated
Inputs may be any that keep to these rules, and one draw needn't show every extreme that they name: `tile_rows`: every slot, used or not, holds a local tile row below 256; used tiles lie on or below the global diagonal. `tile_cols`: every slot holds a local tile column below 128. `tile_counts`: devices on the last block row use all 256 slots.
All inputs are finite; a program needn't handle non-finite values.
Results may differ from a plain program's by a relative error of at most 0.0003.
Values sent between devices are 32-bit elements; how exact they have to be, the bound alone decides.
A program may use at most 64 MiB of HBM per device.

v0:
```python
import jax
import jax.numpy as jnp
from jax import lax
from jax.sharding import PartitionSpec as P


def tile_products(
    tiles, tile_rows, tile_cols, tile_total, row_vec, col_vec, block_size, with_rows, with_cols
):
    vectors = row_vec.shape[0]
    tile_width = tiles.shape[-1]
    row_tiles = row_vec.reshape(vectors, -1, tile_width)
    col_tiles = col_vec.reshape(vectors, -1, tile_width)
    row_blocks = row_tiles.shape[1]
    col_blocks = col_tiles.shape[1]
    offsets = jnp.arange(block_size, dtype=jnp.int32)
    row_range = jnp.arange(row_blocks, dtype=jnp.int32)
    col_range = jnp.arange(col_blocks, dtype=jnp.int32)

    def advance(block_step, carry):
        acc_rows, acc_cols = carry
        first_slot = block_step * block_size
        tile_block = lax.dynamic_slice_in_dim(tiles, first_slot, block_size, 0)
        row_index = lax.dynamic_slice_in_dim(tile_rows, first_slot, block_size, 0)
        col_index = lax.dynamic_slice_in_dim(tile_cols, first_slot, block_size, 0)
        alive_mask = (first_slot + offsets < tile_total).astype(jnp.float32)
        if with_rows:
            picked = jnp.take(col_tiles, col_index, axis=1)
            images = jnp.einsum("vmk,mjk->vmj", picked, tile_block, precision=lax.Precision.HIGHEST)
            one_hot = (row_index[:, None] == row_range[None, :]).astype(jnp.float32) * alive_mask[
                :, None
            ]
            acc_rows = acc_rows + jnp.einsum(
                "vmj,ms->vsj", images, one_hot, precision=lax.Precision.HIGHEST
            )
        if with_cols:
            picked_rows = jnp.take(row_tiles, row_index, axis=1)
            images_back = jnp.einsum(
                "vmj,mjk->vmk", picked_rows, tile_block, precision=lax.Precision.HIGHEST
            )
            one_hot_cols = (col_index[:, None] == col_range[None, :]).astype(
                jnp.float32
            ) * alive_mask[:, None]
            acc_cols = acc_cols + jnp.einsum(
                "vmk,mt->vtk", images_back, one_hot_cols, precision=lax.Precision.HIGHEST
            )
        return (acc_rows, acc_cols)

    block_count = (tile_total + block_size - 1) // block_size
    initial = (
        jnp.zeros((vectors, row_blocks, tile_width), jnp.float32),
        jnp.zeros((vectors, col_blocks, tile_width), jnp.float32),
    )
    acc_rows, acc_cols = lax.fori_loop(0, block_count, advance, initial)
    return (acc_rows.reshape(vectors, -1), acc_cols.reshape(vectors, -1))


def inner_products(left, right):
    return jnp.dot(
        left, right.T, precision=lax.Precision.HIGHEST, preferred_element_type=jnp.float32
    )


def local(tiles, tile_rows, tile_cols, tile_counts, block_now, block_prev, coupling, diag_energy):
    own_tiles = tiles[0, 0]
    own_rows = tile_rows[0, 0]
    own_cols = tile_cols[0, 0]
    tile_total = tile_counts[0, 0]
    slot_count = own_tiles.shape[0]
    block_size = min(32, slot_count // 8)
    row_vec = lax.all_gather(block_now, "col", axis=1, tiled=True)
    col_vec = lax.all_gather(block_now, "row", axis=1, tiled=True)
    part_rows, _ = tile_products(
        own_tiles, own_rows, own_cols, tile_total, row_vec, col_vec, block_size, True, False
    )
    _, part_cols = tile_products(
        own_tiles, own_rows, own_cols, tile_total, row_vec, col_vec, block_size, False, True
    )
    row_sum = lax.psum_scatter(part_rows, "col", scatter_dimension=1, tiled=True)
    col_sum = lax.psum_scatter(part_cols, "row", scatter_dimension=1, tiled=True)
    image = row_sum + col_sum + diag_energy[None, :] * block_now
    total_states = block_now.shape[1] * lax.axis_size("row") * lax.axis_size("col")
    alpha = lax.psum(inner_products(block_now, image), ("row", "col")) / total_states
    residual = (
        image
        - jnp.dot(alpha.T, block_now, precision=lax.Precision.HIGHEST)
        - jnp.dot(coupling, block_prev, precision=lax.Precision.HIGHEST)
    )
    gram_matrix = lax.psum(inner_products(residual, residual), ("row", "col")) / total_states
    factor = jnp.linalg.cholesky(gram_matrix)
    next_block = jax.scipy.linalg.solve_triangular(factor, residual, lower=True)
    return (next_block, alpha, factor.T)


def solution(mesh):
    return jax.shard_map(
        local,
        mesh=mesh,
        in_specs=(
            P("row", "col", None, None, None),
            P("row", "col", None),
            P("row", "col", None),
            P("row", "col"),
            P(None, ("row", "col")),
            P(None, ("row", "col")),
            P(),
            P(("row", "col")),
        ),
        out_specs=(P(None, ("row", "col")), P(), P()),
        check_vma=False,
    )
```

profile of v0, /device:TPU:1, one launch (start us, length us, event | category | flops | bytes accessed | tf_op | source)
XLA Modules:
  0.0 365.0 jit_solution(4885745151350478311)
XLA Ops:
  7.2 0.0 copy-start
  7.2 0.0 all-gather.2.cloned.1.call-start
  7.2 0.7 all-gather.2.cloned.1.call-update
  7.9 0.0 reduce-scatter.3.cloned.1.call-start
  8.6 26.7 %all_gather.6 = f32[8,16384]{1,0:T(8,128)S(1)} all-gather(f32[8,2048]{1,0:T(8,128)} %param.16), channel_id=1, replica_groups=mesh['row'=8,'col'=16] {'row'}, dimensions={1}, use_global_device_ids=true | all-gather | bytes 589824 | tf_op jit(solution)/shard_map/all_gather | solution.py:72
  35.3 0.1 broadcast_in_dim.39
  35.3 9.1 %while.22 = (s32[]{:T(128)}, f32[8,256,128]{2,1,0:T(8,128)S(1)}, s32[]{:T(128)}, s32[256]{0:T(256)}, s32[]{:T(128)}, /*index=5*/f32[256,128,128]{2,1,0:T(8,128)}...) while((s32[]{:T(128)}, f32[8,256,128]{2,1,0:T(8,128)S(1)}, ...), condition=%wide.region_1.2_spmd.clone, body=%wide.region_0.1_spmd.clone.sunk | while | flops 151307552 | bytes 4855159 | solution.py:54
  35.4 1.4 compare_and_fusion.4
  36.8 0.6 gather_fusion
  37.4 5.0 %fusion.72 = f32[32,128,8]{1,2,0:T(8,128)S(1)} fusion(f32[256,128,128]{2,1,0:T(8,128)} %get-tuple-element.338, s32[]{:T(128)S(6)} %select_n.69, f32[32,8,128]{2,1,0:T(8,128)S(1)} %gather_fusion, pred[32]{0:T(512)(128)(4,1)S(1)} %get-tuple-element.296), kind=kOutput, calls=%fused_computation.6.clone.1 | convolution fusion | flops 50364416 | bytes 2359332 | tf_op jit(solution)/shard_map/while/body/vmk,mjk->vmj/dot_general | solution.py:29
  42.3 0.8 dynamic_slice.37
  43.1 1.3 fusion.73
  44.4 0.0 copy-start.1
  44.4 0.0 copy-start.2
  44.4 0.0 copy-start.3
  44.4 1.6 copy.36
  46.0 0.0 reduce-scatter.3.cloned.1.call-update
  46.1 0.0 reduce-scatter.5.cloned.1.call-start
  46.1 12.7 %all-gather.2.cloned.1.call-done = f32[8,32768]{1,0:T(8,128)} async-done(((f32[8,2048]{1,0:T(8,128)}), f32[8,32768]{1,0:T(8,128)}) %all-gather.2.cloned.1.call-update) | async-done | bytes 1048592 | tf_op jit(solution)/shard_map/all_gather | solution.py:71
  58.9 8.3 %while.23 = (s32[]{:T(128)}, f32[8,128,128]{2,1,0:T(8,128)S(1)}, s32[]{:T(128)}, s32[256]{0:T(256)}, s32[]{:T(128)}, /*index=5*/f32[256,128,128]{2,1,0:T(8,128)}...) while((s32[]{:T(128)}, f32[8,128,128]{2,1,0:T(8,128)S(1)}, ...), condition=%wide.region_4.5_spmd.clone, body=%wide.region_3.4_spmd.clone.sunk | while | flops 100836640 | bytes 3806583 | solution.py:54
  58.9 1.4 compare_and_fusion.5
  60.3 1.8 gather_fusion.1
  62.1 3.5 fusion.78
  65.6 0.8 dynamic_slice.39
  66.4 0.8 fusion.79
  67.2 1.1 copy.37
  68.3 0.0 reduce-scatter.5.cloned.1.call-update
  68.3 113.4 %reduce-scatter.3.cloned.1.call-done = f32[8,2048]{1,0:T(8,128)} async-done(((f32[8,32768]{1,0:T(8,128)}), f32[8,2048]{1,0:T(8,128)}) %reduce-scatter.3.cloned.1.call-update) | async-done | bytes 65552 | tf_op jit(solution)/shard_map/reduce_scatter | solution.py:79
  181.7 37.2 %reduce-scatter.5.cloned.1.call-done = f32[8,2048]{1,0:T(8,128)} async-done(((f32[8,16384]{1,0:T(8,128)}), f32[8,2048]{1,0:T(8,128)}) %reduce-scatter.5.cloned.1.call-update) | async-done | bytes 65552 | tf_op jit(solution)/shard_map/reduce_scatter | solution.py:80
  218.9 0.0 copy-done.1
  218.9 0.0 copy-done.2
  218.9 1.1 convolution_bitcast_fusion.2
  220.0 68.0 %psum.14 = f32[8,8]{0,1:T(8,128)S(1)} all-reduce(f32[8,8]{0,1:T(8,128)S(1)} %convolution_bitcast_fusion.2), channel_id=1, replica_groups=mesh['row'=8,'col'=16] {'row','col'}, use_global_device_ids=true, to_apply=%region_6.7 | all-reduce | flops 64 | bytes 512 | tf_op jit(solution)/shard_map/psum | solution.py:83
  288.0 1.1 convolution_subtract_fusion.1
  289.0 0.0 copy-done
  289.0 0.0 copy-done.3
  289.0 0.2 convolution_subtract_fusion
  289.2 0.2 fusion.48
  289.4 64.1 %psum.15 = f32[8,8]{0,1:T(8,128)S(1)} all-reduce(f32[8,8]{0,1:T(8,128)S(1)} %fusion.48), channel_id=1, replica_groups=mesh['row'=8,'col'=16] {'row','col'}, use_global_device_ids=true, to_apply=%region_7.8 | all-reduce | flops 64 | bytes 512 | tf_op jit(solution)/shard_map/psum | solution.py:89
  353.5 0.1 copy.17
  353.6 0.7 cholesky.16
  354.4 0.6 compare_reduce_fusion
  355.0 0.6 fusion.47
  355.7 0.6 custom-call.7
  356.3 0.9 fusion.44
  357.2 0.7 copy.20
  357.8 0.7 copy.19
  (7 shorter events, 0.1 us)
Async XLA Ops:
  7.2 281.9 %copy-start = (f32[8,2048]{1,0:T(8,128)S(1)}, f32[8,2048]{1,0:T(8,128)}, u32[]{:S(2)}) copy-start(f32[8,2048]{1,0:T(8,128)} %param.17) | copy-start | bytes 196612
  7.2 51.7 %all-gather.2.cloned.1.call-start = ((), (), s32[]{:S(2)}) async-start(), calls=%async_computation.3 | async-start | bytes 1114112 | tf_op jit(solution)/shard_map/all_gather | solution.py:71
  7.9 173.8 %reduce-scatter.3.cloned.1.call-start = ((), (), s32[]{:S(2)}) async-start(), calls=%async_computation.2 | async-start | bytes 1114112 | tf_op jit(solution)/shard_map/reduce_scatter | solution.py:79
  44.4 174.5 %copy-start.1 = (f32[8,2048]{1,0:T(8,128)S(1)}, f32[8,2048]{1,0:T(8,128)}, u32[]{:S(2)}) copy-start(f32[8,2048]{1,0:T(8,128)} %param.16) | copy-start | bytes 196612
  44.4 174.5 %copy-start.2 = (f32[2048]{0:T(1024)S(1)}, f32[2048]{0:T(1024)}, u32[]{:S(2)}) copy-start(f32[2048]{0:T(1024)} %param.19) | copy-start | bytes 24580
  44.4 244.6 %copy-start.3 = (f32[8,8]{1,0:T(8,128)S(1)}, f32[8,8]{1,0:T(8,128)}, u32[]{:S(2)}) copy-start(f32[8,8]{1,0:T(8,128)} %param.18) | copy-start | bytes 772
  46.1 172.9 %reduce-scatter.5.cloned.1.call-start = ((), (), s32[]{:S(2)}) async-start(), calls=%async_computation.4 | async-start | bytes 589824 | tf_op jit(solution)/shard_map/reduce_scatter | solution.py:80
Sparse Core Ops, SparseCore 0:
  10.4 48.3 all-gather.1
  62.7 118.9 reduce-scatter.2
  184.1 34.7 reduce-scatter.4
where the time goes:
time: 367 us; the launch traced here: 365 us
  waiting for transfers between devices  164 us (45%)
  blocking collectives  159 us (43%)
  between operations  14.5 us (4%)
  matrix products  13.9 us (4%)
  local copies, waits for them, and re-layouts  8.15 us (2%)
  other arithmetic  5.5 us (1%)
    reduce_scatter x1, waiting for transfers between devices, local(): lax.psum_scatter(part_rows, 'col', scatter_dimension=1, tiled=True)  113 us
    psum x1, blocking collectives, local(): lax.psum(inner_products(block_now, image), ('row', 'col')) / total_states  68 us
    psum x1, blocking collectives, local(): lax.psum(inner_products(residual, residual), ('row', 'col')) / total_states  64.1 us
    reduce_scatter x1, waiting for transfers between devices, local(): lax.psum_scatter(part_cols, 'row', scatter_dimension=1, tiled=True)  37.2 us
    all_gather x1, blocking collectives, local(): col_vec = lax.all_gather(block_now, 'row', axis=1, tiled=True)  26.7 us
    all_gather x1, waiting for transfers between devices, local(): row_vec = lax.all_gather(block_now, 'col', axis=1, tiled=True)  12.7 us
  transfers between devices with their start and end apart: 3, of which 3 were waited for; matrix products, arithmetic and copies ran while one was open for 5% of the time, Pallas kernels for 0%

commit v1 on v0

v1 whole, which is shorter than its diff:
```python
import functools

import jax
import jax.numpy as jnp
from jax import lax
from jax.experimental import pallas as pl
from jax.experimental.pallas import tpu as pltpu
from jax.sharding import PartitionSpec as P

MESH = pl.DeviceIdType.MESH
NT_DIMS = (((1,), (1,)), ((), ()))
NN_DIMS = (((1,), (0,)), ((), ()))
F32 = jnp.float32
BF16 = jnp.bfloat16
HIGHEST = lax.Precision.HIGHEST
CHUNK = 16


def dot_exact(left, right, dims):
    return lax.dot_general(left, right, dims, precision=HIGHEST, preferred_element_type=F32)


def split_rows(value):
    high = value.astype(BF16).astype(F32)
    return jnp.concatenate([high, value - high], axis=0).astype(BF16)


def kernel(
    total_states,
    tiles,
    rows_s,
    cols_s,
    count_s,
    rows_v,
    cols_v,
    now,
    prev,
    coupling,
    diag,
    next_out,
    alpha_out,
    beta_out,
    tile_f32,
    tile_hi,
    tile_lo,
    col_vec,
    row_vec,
    col_split,
    row_split,
    images,
    part_rows,
    part_cols,
    row_pair,
    row_ring,
    row_sum,
    row_last,
    col_ring,
    col_sum,
    col_last,
    image,
    resid,
    red_send,
    red_one,
    red_two,
    tile_sem,
    send_sem,
    col_sem,
    row_sem,
    pair_sem,
    ring_sem,
    last_sem,
    one_sem,
    two_sem,
):
    r = lax.axis_index("row")
    c = lax.axis_index("col")
    z, ylo = r // 2, r % 2
    yhi, x, core = c // 8, (c // 2) % 4, c % 2
    slots = tiles.shape[0]
    width = now.shape[1]

    def row_of(zz, yy):
        return zz * 2 + yy

    def col_of(yy, xx, cc):
        return yy * 8 + xx * 2 + cc

    zs = [(z + d) % 4 for d in range(1, 4)]
    xs = [(x + d) % 4 for d in range(1, 4)]
    row_peer = row_of(z, 1 - ylo)
    col_peer = col_of(1 - yhi, x, core)
    pair = col_of(yhi, x, 1 - core)

    chunks = slots // CHUNK

    def tile_copy(i):
        part = pl.ds(i * CHUNK, CHUNK)
        return pltpu.make_async_copy(tiles.at[part], tile_f32.at[part], tile_sem.at[i])

    for i in range(chunks):
        tile_copy(i).start()

    group_one = [(r, col_of(yhi, (x + d // 2) % 4, (core + d) % 2)) for d in range(1, 8)]
    group_two = [
        (row_of((z + d // 4) % 4, (ylo + d // 2) % 2), col_of((yhi + d) % 2, x, core))
        for d in range(1, 16)
    ]
    barrier = pltpu.get_barrier_semaphore()
    for peer in group_one + group_two:
        pl.semaphore_signal(barrier, inc=1, device_id=peer, device_id_type=MESH)

    def piece(ref, p):
        return ref.at[:, pl.ds(pl.multiple_of(p * width, width), width)]

    piece(col_vec, r)[...] = now[...]
    piece(row_vec, c)[...] = now[...]
    pl.semaphore_wait(barrier, len(group_one) + len(group_two))

    sends = []

    def send(src, dst, recv, peer):
        copy = pltpu.make_async_remote_copy(
            src_ref=src,
            dst_ref=dst,
            send_sem=send_sem.at[len(sends)],
            recv_sem=recv,
            device_id=peer,
            device_id_type=MESH,
        )
        copy.start()
        sends.append(copy)

    def arrived(dst, recv, peer):
        pltpu.make_async_remote_copy(
            src_ref=dst,
            dst_ref=dst,
            send_sem=send_sem.at[0],
            recv_sem=recv,
            device_id=peer,
            device_id_type=MESH,
        ).wait_recv()

    send(now, piece(col_vec, r), col_sem.at[r], (row_peer, c))
    send(now, piece(row_vec, c), row_sem.at[c], (r, col_peer))
    for zz in zs:
        send(now, piece(col_vec, r), col_sem.at[r], (row_of(zz, ylo), c))
    for xx in xs:
        send(now, piece(row_vec, c), row_sem.at[c], (r, col_of(yhi, xx, core)))
    send(now, piece(row_vec, c), row_sem.at[c], (r, pair))

    def convert(first, last):
        def chunk(i, _):
            tile_copy(i).wait()

            def one(j, _):
                value = tile_f32[i * CHUNK + j]
                high = value.astype(BF16)
                tile_hi[i * CHUNK + j] = high
                tile_lo[i * CHUNK + j] = (value - high.astype(F32)).astype(BF16)
                return 0

            lax.fori_loop(0, CHUNK, one, 0, unroll=4)
            return 0

        lax.fori_loop(first, last, chunk, 0)

    convert(0, 6)
    arrived(piece(col_vec, row_peer), col_sem.at[row_peer], (row_peer, c))
    for zz in zs:
        send(
            piece(col_vec, row_peer), piece(col_vec, row_peer), col_sem.at[row_peer], (row_of(zz, ylo), c)
        )
    arrived(piece(row_vec, col_peer), row_sem.at[col_peer], (r, col_peer))
    for xx in xs:
        send(
            piece(row_vec, col_peer),
            piece(row_vec, col_peer),
            row_sem.at[col_peer],
            (r, col_of(yhi, xx, core)),
        )
    send(piece(row_vec, col_peer), piece(row_vec, col_peer), row_sem.at[col_peer], (r, pair))
    convert(6, 10)

    def relay(yy):
        for xx in xs:
            p = col_of(yy, xx, core)
            arrived(piece(row_vec, p), row_sem.at[p], (r, col_of(yhi, xx, core)))
            send(piece(row_vec, p), piece(row_vec, p), row_sem.at[p], (r, pair))

    relay(yhi)
    convert(10, chunks)
    relay(1 - yhi)
    for yy in (ylo, 1 - ylo):
        for zz in zs:
            p = row_of(zz, yy)
            arrived(piece(col_vec, p), col_sem.at[p], (row_of(zz, ylo), c))

    def split_vectors(src, dst):
        def one(t, _):
            dst[t] = split_rows(src[:, pl.ds(pl.multiple_of(t * 128, 128), 128)])
            return 0

        lax.fori_loop(0, dst.shape[0], one, 0, unroll=8)

    split_vectors(col_vec, col_split)

    def products(first, last, index, vectors, transposed):
        unroll = 8

        def body(g, _):
            for u in range(unroll):
                m = g * unroll + u
                left = vectors[index[m]]
                if transposed:
                    weights = jnp.concatenate([tile_hi[m], tile_lo[m]], axis=0)
                    out = lax.dot_general(left, weights, NT_DIMS, preferred_element_type=F32)
                else:
                    weights = jnp.concatenate([tile_hi[m], tile_lo[m]], axis=1)
                    out = lax.dot_general(left, weights, NN_DIMS, preferred_element_type=F32)
                total = (out[0:8, 0:128] + out[8:16, 0:128]) + out[0:8, 128:256]
                images[pl.ds(m, 8, stride=slots), :] = total
            return 0

        lax.fori_loop(first // unroll, last // unroll, body, 0)

    used = lax.broadcasted_iota(jnp.int32, (1, slots), 1) < count_s[0, 0]

    def scatter(place, dst):
        count = dst.shape[1]
        wanted = jnp.where(used, place, -1)
        pick = (
            (lax.broadcasted_iota(jnp.int32, (count, slots), 0) == wanted).astype(F32).astype(BF16)
        )

        def one(v, _):
            value = images[pl.ds(pl.multiple_of(v * slots, slots), slots), :]
            high = value.astype(BF16)
            low = (value - high.astype(F32)).astype(BF16)
            out = lax.dot_general(
                pick, jnp.concatenate([high, low], axis=1), NN_DIMS, preferred_element_type=F32
            )
            dst[v] = out[:, 0:128] + out[:, 128:256]
            return 0

        lax.fori_loop(0, 8, one, 0)

    products(0, slots, cols_s, col_split, True)
    place = rows_v[...]
    owner = place // 16
    place = ((owner % 2) * 8 + ((owner // 2) % 4) * 2 + owner // 8) * 16 + place % 16
    scatter(place, part_rows)
    half = part_rows.shape[1] // 2

    def half_of(cc):
        return part_rows.at[:, pl.ds(pl.multiple_of(cc * half, half), half), :]

    send(half_of(1 - core), row_pair, pair_sem.at[0], (r, pair))

    for yy in (yhi, 1 - yhi):
        for xx in [x] + xs:
            if yy is yhi and xx is x:
                p = col_of(yhi, x, 1 - core)
            else:
                p = col_of(yy, xx, 1 - core)
            arrived(piece(row_vec, p), row_sem.at[p], (r, pair))
    split_vectors(row_vec, row_split)
    mid = slots // 4
    products(0, mid, rows_s, row_split, False)

    arrived(row_pair, pair_sem.at[0], (r, pair))
    mine = half_of(core)

    def add_pair(v, _):
        row_pair[v] = row_pair[v] + mine[v]
        return 0

    lax.fori_loop(0, 8, add_pair, 0)
    for d, xx in enumerate(xs):
        send(
            row_pair.at[:, pl.ds(pl.multiple_of(xx * 32, 32), 32), :],
            row_ring.at[d],
            ring_sem.at[d],
            (r, col_of(yhi, xx, core)),
        )
    products(mid, slots, rows_s, row_split, False)
    scatter(cols_v[...], part_cols)
    for d, zz in enumerate(zs):
        send(
            part_cols.at[:, pl.ds(pl.multiple_of(zz * 32, 32), 32), :],
            col_ring.at[d],
            ring_sem.at[3 + d],
            (row_of(zz, ylo), c),
        )

    flat_rows = part_rows.reshape(8 * part_rows.shape[1], 128)
    stride = part_rows.shape[1]

    def inner(q, acc):
        owner = (q % 2) * 8 + ((q // 2) % 4) * 2 + q // 8
        left = jnp.concatenate([row_split[owner * 16 + t] for t in range(16)], axis=1)
        right = jnp.concatenate(
            [split_rows(flat_rows[pl.ds(q * 16 + t, 8, stride=stride), :]) for t in range(16)], axis=1
        )
        return acc + lax.dot_general(left, right, NT_DIMS, preferred_element_type=F32)

    both = lax.fori_loop(0, 16, inner, jnp.zeros((16, 16), F32))
    cross = (both[0:8, 0:8] + both[8:16, 0:8]) + both[0:8, 8:16]
    eye = (
        lax.broadcasted_iota(jnp.int32, (8, 8), 0) == lax.broadcasted_iota(jnp.int32, (8, 8), 1)
    ).astype(F32)

    def diag_of(t):
        return diag[t : t + 1, :]

    def now_of(t):
        return now[:, t * 128 : (t + 1) * 128]

    count = width // 128
    weighted = jnp.concatenate([now_of(t) * diag_of(t) for t in range(count)], axis=1)
    cross = cross + dot_exact(eye, cross, NT_DIMS) + dot_exact(now[...], weighted, NT_DIMS)

    def reduce_send(k, value):
        red_send[k, :, 0:8] = value
        slot = x * 2 + core
        red_one[k, slot, :, 0:8] = value
        for peer in group_one:
            send(red_send.at[k], red_one.at[k, slot], one_sem.at[k, slot], peer)

    def reduce_pass(k):
        for d in range(1, 8):
            slot = ((x + d // 2) % 4) * 2 + (core + d) % 2
            arrived(red_one.at[k, slot], one_sem.at[k, slot], group_one[d - 1])
        total = red_one[k, 0, :, 0:8]
        for i in range(1, 8):
            total = total + red_one[k, i, :, 0:8]
        red_send[2 + k, :, 0:8] = total
        slot = r * 2 + yhi
        red_two[k, slot, :, 0:8] = total
        for peer in group_two:
            send(red_send.at[2 + k], red_two.at[k, slot], two_sem.at[k, slot], peer)

    def reduce_end(k):
        for d in range(1, 16):
            slot = row_of((z + d // 4) % 4, (ylo + d // 2) % 2) * 2 + (yhi + d) % 2
            arrived(red_two.at[k, slot], two_sem.at[k, slot], group_two[d - 1])
        total = red_two[k, 0, :, 0:8]
        for i in range(1, 16):
            total = total + red_two[k, i, :, 0:8]
        return total

    red_send[...] = jnp.zeros_like(red_send)
    reduce_send(0, cross)

    def ring_total(own, own_at, ring, base, dst, peers):
        for d in range(3):
            arrived(ring.at[d], ring_sem.at[base + d], peers[d])

        def one(v, _):
            own_part = own[v, pl.ds(pl.multiple_of(own_at * 32, 32), 32), :]
            dst[v] = (own_part + ring[0, v]) + (ring[1, v] + ring[2, v])
            return 0

        lax.fori_loop(0, 8, one, 0)

    def lot(ref, k):
        return ref.at[:, pl.ds(pl.multiple_of(k * 16, 16), 16), :]

    row_from = [(r, col_of(yhi, (x + 3 - d) % 4, core)) for d in range(3)]
    col_from = [(row_of((z + 3 - d) % 4, ylo), c) for d in range(3)]
    ring_total(row_pair, x, row_ring, 0, row_sum, row_from)
    send(lot(row_sum, 1 - yhi), row_last, last_sem.at[0], (r, col_peer))
    reduce_pass(0)
    ring_total(part_cols, z, col_ring, 3, col_sum, col_from)
    send(lot(col_sum, 1 - ylo), col_last, last_sem.at[1], (row_peer, c))
    scale = 1.0 / total_states
    alpha = reduce_end(0) * scale
    alpha_out[...] = alpha
    alpha_t = dot_exact(eye, alpha, NT_DIMS)
    taken = dot_exact(alpha_t, now[...], NN_DIMS) + dot_exact(coupling[...], prev[...], NN_DIMS)

    arrived(row_last, last_sem.at[0], (r, col_peer))
    arrived(col_last, last_sem.at[1], (row_peer, c))
    row_mine, col_mine = lot(row_sum, yhi), lot(col_sum, ylo)
    for v in range(8):
        image[v * 16 : (v + 1) * 16, :] = (row_mine[v] + row_last[v]) + (col_mine[v] + col_last[v])
    for t in range(count):
        value = image[pl.ds(t, 8, stride=16), :] + diag_of(t) * now_of(t)
        resid[:, t * 128 : (t + 1) * 128] = value - taken[:, t * 128 : (t + 1) * 128]
    residual = resid[...]
    reduce_send(1, dot_exact(residual, residual, NT_DIMS))
    reduce_pass(1)
    gram = reduce_end(1) * scale

    work = jnp.concatenate([gram, eye], axis=1)
    line = lax.broadcasted_iota(jnp.int32, (8, 16), 0)
    for j in range(8):
        lead = jnp.broadcast_to(work[j : j + 1, :], (8, 16))
        column = jnp.broadcast_to(work[:, j : j + 1], (8, 16))
        pivot = jnp.broadcast_to(work[j : j + 1, j : j + 1], (8, 16))
        root = jnp.sqrt(pivot)
        scaled = lead / root
        work = jnp.where(
            line == j, scaled, jnp.where(line > j, work - (column / root) * scaled, work)
        )
    upper = lax.broadcasted_iota(jnp.int32, (8, 8), 0) <= lax.broadcasted_iota(jnp.int32, (8, 8), 1)
    beta_out[...] = jnp.where(upper, work[:, 0:8], 0.0)
    next_out[...] = dot_exact(work[:, 8:16], residual, NN_DIMS)

    for copy in sends:
        copy.wait_send()


def local(tiles, tile_rows, tile_cols, tile_counts, block_now, block_prev, coupling, diag_energy):
    slots, tile_width = tiles.shape[2], tiles.shape[3]
    vectors, width = block_now.shape
    n_row, n_col = lax.axis_size("row"), lax.axis_size("col")
    count = width // tile_width
    rows, cols = tile_rows.reshape(1, slots), tile_cols.reshape(1, slots)
    vmem = pl.BlockSpec(memory_space=pltpu.VMEM)
    smem = pl.BlockSpec(memory_space=pltpu.SMEM)
    dma = pltpu.SemaphoreType.DMA
    n_rt, n_ct = n_col * count, n_row * count
    shape = jax.ShapeDtypeStruct
    return pl.pallas_call(
        functools.partial(kernel, width * n_row * n_col),
        out_shape=(shape((vectors, width), F32), shape((8, 8), F32), shape((8, 8), F32)),
        in_specs=[pl.BlockSpec(memory_space=pl.ANY), smem, smem, smem, vmem, vmem, vmem, vmem, vmem, vmem],
        out_specs=(vmem, vmem, vmem),
        scratch_shapes=[
            pltpu.VMEM((slots, tile_width, tile_width), F32),
            pltpu.VMEM((slots, tile_width, tile_width), BF16),
            pltpu.VMEM((slots, tile_width, tile_width), BF16),
            pltpu.VMEM((vectors, n_row * width), F32),
            pltpu.VMEM((vectors, n_col * width), F32),
            pltpu.VMEM((n_ct, 16, tile_width), BF16),
            pltpu.VMEM((n_rt, 16, tile_width), BF16),
            pltpu.VMEM((vectors * slots, tile_width), F32),
            pltpu.VMEM((vectors, n_rt, tile_width), F32),
            pltpu.VMEM((vectors, n_ct, tile_width), F32),
            pltpu.VMEM((vectors, n_rt // 2, tile_width), F32),
            pltpu.VMEM((3, vectors, 2 * count, tile_width), F32),
            pltpu.VMEM((vectors, 2 * count, tile_width), F32),
            pltpu.VMEM((vectors, count, tile_width), F32),
            pltpu.VMEM((3, vectors, 2 * count, tile_width), F32),
            pltpu.VMEM((vectors, 2 * count, tile_width), F32),
            pltpu.VMEM((vectors, count, tile_width), F32),
            pltpu.VMEM((vectors * count, tile_width), F32),
            pltpu.VMEM((vectors, width), F32),
            pltpu.VMEM((4, 8, 128), F32),
            pltpu.VMEM((2, 8, 8, 128), F32),
            pltpu.VMEM((2, 16, 8, 128), F32),
            dma((slots // CHUNK,)),
            dma((80,)),
            dma((n_row,)),
            dma((n_col,)),
            dma((1,)),
            dma((6,)),
            dma((2,)),
            dma((2, 8)),
            dma((2, 16)),
        ],
        compiler_params=pltpu.CompilerParams(
            collective_id=0, has_side_effects=True, vmem_limit_bytes=60 * 2**20
        ),
    )(
        tiles.reshape(slots, tile_width, tile_width),
        rows.reshape(slots),
        cols.reshape(slots),
        tile_counts,
        rows,
        cols,
        block_now,
        block_prev,
        coupling,
        diag_energy.reshape(count, tile_width),
    )


def solution(mesh):
    return jax.shard_map(
        local,
        mesh=mesh,
        in_specs=(
            P("row", "col", None, None, None),
            P("row", "col", None),
            P("row", "col", None),
            P("row", "col"),
            P(None, ("row", "col")),
            P(None, ("row", "col")),
            P(),
            P(("row", "col")),
        ),
        out_specs=(P(None, ("row", "col")), P(), P()),
        check_vma=False,
    )
```

time: 367 us -> 66.9 us (0.18)
  waiting for transfers between devices: 164 us -> 0 us
  blocking collectives: 159 us -> 0 us
  Pallas kernels: 0 us -> 61.3 us
  matrix products: 13.9 us -> 0 us
  between operations: 14.5 us -> 1.29 us
  other arithmetic: 5.5 us -> 0 us
  local copies, waits for them, and re-layouts: 8.15 us -> 4.02 us
    reduce_scatter x2 -> x0, waiting for transfers between devices: 151 us -> none  [the longest x1 113 us: local(): lax.psum_scatter(part_rows, 'col', scatter_dimension=1, tiled=True)]
    psum x2 -> x0, blocking collectives: 132 us -> none  [the longest x1 68 us: local(): lax.psum(inner_products(block_now, image), ('row', 'col')) / total_states]
    pallas_call x0 -> x1, Pallas kernels: none -> 61.3 us  [local(): pl.pallas_call(functools.partial(kernel, width * n_row * n_col), out_shap...]
    all_gather x1 -> x0, blocking collectives: 26.7 us -> none  [local(): col_vec = lax.all_gather(block_now, 'row', axis=1, tiled=True)]
    dot_general x8 -> x0, matrix products: 13 us -> none  [the longest x1 4.97 us: advance(): jnp.einsum('vmk,mjk->vmj', picked, tile_block, precision=lax.Precision.HI...]
    all_gather x1 -> x0, waiting for transfers between devices: 12.7 us -> none  [local(): row_vec = lax.all_gather(block_now, 'col', axis=1, tiled=True)]
  transfers between devices with their start and end apart: 3 -> 0, of which waited for: 3 -> 0; matrix products, arithmetic and copies ran while one was open for 5% -> 0% of each run, Pallas kernels for 0% -> 0%
where the time goes in v1:
time: 66.9 us; the launch traced here: 66.6 us
  Pallas kernels  61.3 us (92%)
  local copies, waits for them, and re-layouts  4.02 us (6%)
  between operations  1.29 us (2%)
    pallas_call x1, Pallas kernels, local(): pl.pallas_call(functools.partial(kernel, width * n_row * n_col), out_shap...  61.3 us
    unnamed x3, local copies, waits for them, and re-layouts  4.02 us

profile of v1, /device:TPU:1, one launch (start us, length us, event | category | flops | bytes accessed | tf_op | source)
XLA Modules:
  0.0 66.6 jit_solution(18329823187923538604)
XLA Ops:
  1.3 61.3 %shard_map.103 = (f32[8,2048]{1,0:T(8,128)}, f32[8,8]{1,0:T(8,128)}, f32[8,8]{1,0:T(8,128)}) custom-call(f32[256,128,128]{2,1,0:T(8,128)} %bitcast.6, s32[256]{0:T(256)} %bitcast.8, s32[256]{0:T(256)} %bitcast.10, s32[1,1]{1,0:T(1,128)S(6)} %copy.14.count_s, s32[1,256]{1,0:T(1,128)} %bitcast.9, s32[1,256]{1,0:T(1,128)} %bitcast.11, f32[8,2048]{1,0:T(8,128)} %now.1, ...), custom_call_target="tpu_custom_call" | custom-call | tf_op jit(solution)/shard_map/pallas_call | solution.py:424
  62.6 1.5 %copy.15 = f32[8,2048]{1,0:T(8,128)} copy(f32[8,2048]{1,0:T(8,128)} %get-tuple-element.6) | data formatting | bytes 131072
  64.0 1.3 %copy.16 = f32[8,8]{1,0:T(8,128)} copy(f32[8,8]{1,0:T(8,128)} %get-tuple-element.7) | data formatting | bytes 512
  65.3 1.3 %copy.17 = f32[8,8]{1,0:T(8,128)} copy(f32[8,8]{1,0:T(8,128)} %get-tuple-element.8) | data formatting | bytes 512

commit v2 on v1

v2 whole, which is shorter than its diff:
```python
import functools
import itertools

import jax
import jax.numpy as jnp
from jax import lax
from jax.experimental import pallas as pl
from jax.experimental.pallas import tpu as pltpu
from jax.sharding import PartitionSpec as P

MESH = pl.DeviceIdType.MESH
NT_DIMS = (((1,), (1,)), ((), ()))
NN_DIMS = (((1,), (0,)), ((), ()))
F32 = jnp.float32
BF16 = jnp.bfloat16
HIGHEST = lax.Precision.HIGHEST
CHUNK = 16
UNROLL = 64
SHIFT = 2.5


def dot_exact(left, right, dims):
    return lax.dot_general(left, right, dims, precision=HIGHEST, preferred_element_type=F32)


def split_rows(value):
    high = value.astype(BF16).astype(F32)
    return jnp.concatenate([high, value - high], axis=0).astype(BF16)


def iota(shape, axis):
    return lax.broadcasted_iota(jnp.int32, shape, axis)


def kernel(
    tiles,
    rows_h,
    cols_h,
    count_h,
    rows_w,
    cols_w,
    now_h,
    prev_h,
    diag_h,
    shifted_out,
    early_out,
    final_out,
    tile_f32,
    tile_hi,
    tile_lo,
    rows_s,
    cols_s,
    count_s,
    rows_v,
    cols_v,
    lanczos,
    diag,
    col_vec,
    row_vec,
    col_split,
    row_split,
    images,
    part_rows,
    part_cols,
    row_pair,
    row_ring,
    row_sum,
    row_last,
    col_near,
    col_far,
    col_send,
    col_last,
    image,
    shifted,
    early_send,
    early_one,
    early_two,
    final_send,
    final_all,
    final_sum,
    tile_sem,
    in_sem,
    send_sem,
    col_sem,
    row_sem,
    pair_sem,
    ring_sem,
    last_sem,
    back_sem,
    one_sem,
    two_sem,
    all_sem,
):
    r = lax.axis_index("row")
    c = lax.axis_index("col")
    z, ylo = r // 2, r % 2
    yhi, x, core = c // 8, (c // 2) % 4, c % 2
    slots = tiles.shape[0]
    width = now_h.shape[1]
    count = width // 128
    open_scope = []

    def phase(name):
        if open_scope:
            open_scope.pop().__exit__(None, None, None)
        if name:
            open_scope.append(jax.named_scope(name))
            open_scope[0].__enter__()

    def row_of(zz, yy):
        return zz * 2 + yy

    def col_of(yy, xx, cc):
        return yy * 8 + xx * 2 + cc

    zs = [(z + d) % 4 for d in (2, 1, 3)]
    xs = [(x + d) % 4 for d in (2, 1, 3)]
    row_peer = row_of(z, 1 - ylo)
    col_peer = col_of(1 - yhi, x, core)
    pair = col_of(yhi, x, 1 - core)
    zn = zs[1:]
    far = (row_of(zs[0], 1 - ylo), c)
    col_steps = [(2, 1), (1, 1), (3, 1), (2, 0), (0, 1), (1, 0), (3, 0)]
    col_group = [(row_of((z + a) % 4, (ylo + b) % 2), c) for a, b in col_steps]
    col_back = [(row_of((z + 4 - a) % 4, (ylo + b) % 2), c) for a, b in col_steps]

    phase("start")
    barrier = pltpu.get_barrier_semaphore()
    first_peers = [(row_peer, c), (r, col_peer), far] + [(row_of(zz, ylo), c) for zz in zs]
    first_peers += [(r, col_of(yhi, xx, core)) for xx in xs] + [(r, pair)]
    for peer in first_peers:
        pl.semaphore_signal(barrier, inc=1, device_id=peer, device_id_type=MESH)

    now, prev = lanczos.at[0:8], lanczos.at[8:16]
    loads = [
        pltpu.make_async_copy(src, dst, in_sem.at[i])
        for i, (src, dst) in enumerate(
            [
                (now_h, now),
                (prev_h, prev),
                (diag_h, diag),
                (rows_h, rows_s),
                (cols_h, cols_s),
                (count_h, count_s),
                (rows_w, rows_v),
                (cols_w, cols_v),
            ]
        )
    ]
    loads[0].start()
    chunks = slots // CHUNK

    def tile_copy(i):
        part = pl.ds(i * CHUNK, CHUNK)
        return pltpu.make_async_copy(tiles.at[part], tile_f32.at[part], tile_sem.at[i])

    def piece(ref, p):
        return ref.at[:, pl.ds(pl.multiple_of(p * width, width), width)]

    loads[0].wait()
    for i in range(chunks):
        tile_copy(i).start()
    for copy in loads[1:]:
        copy.start()
    phase("barrier")
    pl.semaphore_wait(barrier, len(first_peers))

    sends = []

    def send(src, dst, recv, peer):
        copy = pltpu.make_async_remote_copy(
            src_ref=src,
            dst_ref=dst,
            send_sem=send_sem.at[len(sends)],
            recv_sem=recv,
            device_id=peer,
            device_id_type=MESH,
        )
        copy.start()
        sends.append(copy)

    def arrived(dst, recv, peer):
        pltpu.make_async_remote_copy(
            src_ref=dst,
            dst_ref=dst,
            send_sem=send_sem.at[0],
            recv_sem=recv,
            device_id=peer,
            device_id_type=MESH,
        ).wait_recv()

    phase("send1")
    send(now, piece(col_vec, r), col_sem.at[r], (row_peer, c))
    send(now, piece(row_vec, c), row_sem.at[c], (r, col_peer))
    send(now, piece(col_vec, r), col_sem.at[r], far)
    for zz in zs:
        send(now, piece(col_vec, r), col_sem.at[r], (row_of(zz, ylo), c))
    for xx in xs:
        send(now, piece(row_vec, c), row_sem.at[c], (r, col_of(yhi, xx, core)))
    send(now, piece(row_vec, c), row_sem.at[c], (r, pair))
    piece(col_vec, r)[...] = now[...]
    piece(row_vec, c)[...] = now[...]

    def convert(first, last):
        def chunk(i, _):
            tile_copy(i).wait()

            def one(j, _):
                value = tile_f32[i * CHUNK + j]
                high = value.astype(BF16)
                tile_hi[i * CHUNK + j] = high
                tile_lo[i * CHUNK + j] = (value - high.astype(F32)).astype(BF16)
                return 0

            lax.fori_loop(0, CHUNK, one, 0, unroll=8)
            return 0

        lax.fori_loop(first, last, chunk, 0)

    phase("conv1")
    convert(0, 9)
    phase("fwdrow")
    arrived(piece(col_vec, row_peer), col_sem.at[row_peer], (row_peer, c))
    for zz in zn:
        send(
            piece(col_vec, row_peer), piece(col_vec, row_peer), col_sem.at[row_peer], (row_of(zz, ylo), c)
        )
    phase("fwdcol")
    arrived(piece(row_vec, col_peer), row_sem.at[col_peer], (r, col_peer))
    for xx in xs:
        send(
            piece(row_vec, col_peer),
            piece(row_vec, col_peer),
            row_sem.at[col_peer],
            (r, col_of(yhi, xx, core)),
        )
    send(piece(row_vec, col_peer), piece(row_vec, col_peer), row_sem.at[col_peer], (r, pair))
    phase("conv2")
    convert(9, chunks)
    for copy in loads[1:]:
        copy.wait()
    phase("early")
    early_send[...] = jnp.zeros_like(early_send)
    known = lanczos[...]
    early_send[0, :, 0:16] = dot_exact(known, known, NT_DIMS)

    phase("waitcolvec")
    for zz in zn:
        for yy in (ylo, 1 - ylo):
            p = row_of(zz, yy)
            arrived(piece(col_vec, p), col_sem.at[p], (row_of(zz, ylo), c))
    for p in (row_of(zs[0], ylo), far[0]):
        arrived(piece(col_vec, p), col_sem.at[p], (p, c))

    def split_vectors(src, dst):
        def one(t, _):
            dst[t] = split_rows(src[:, pl.ds(pl.multiple_of(t * 128, 128), 128)])
            return 0

        lax.fori_loop(0, dst.shape[0], one, 0, unroll=16)

    phase("split1")
    split_vectors(col_vec, col_split)

    def products(first, last, index, vectors, transposed):
        def body(g, _):
            for u in range(UNROLL):
                m = g * UNROLL + u
                left = vectors[index[m]]
                if transposed:
                    weights = jnp.concatenate([tile_hi[m], tile_lo[m]], axis=0)
                    out = lax.dot_general(left, weights, NT_DIMS, preferred_element_type=F32)
                else:
                    weights = jnp.concatenate([tile_hi[m], tile_lo[m]], axis=1)
                    out = lax.dot_general(left, weights, NN_DIMS, preferred_element_type=F32)
                total = (out[0:8, 0:128] + out[8:16, 0:128]) + out[0:8, 128:256]
                images[pl.ds(m, 8, stride=slots), :] = total
            return 0

        lax.fori_loop(first // UNROLL, last // UNROLL, body, 0)

    used = iota((1, slots), 1) < count_s[0, 0]

    def scatter(place, dst):
        wanted = jnp.where(used, place, -1)
        pick = (iota((dst.shape[1], slots), 0) == wanted).astype(F32).astype(BF16)
        for v in range(8):
            value = images[v * slots : (v + 1) * slots, :]
            high = value.astype(BF16)
            low = (value - high.astype(F32)).astype(BF16)
            out = lax.dot_general(
                pick, jnp.concatenate([high, low], axis=1), NN_DIMS, preferred_element_type=F32
            )
            dst[v] = out[:, 0:128] + out[:, 128:256]

    phase("prodrows1")
    products(0, 2 * UNROLL, cols_s, col_split, True)
    phase("relay")
    for yy in (yhi, 1 - yhi):
        for xx in xs:
            p = col_of(yy, xx, core)
            arrived(piece(row_vec, p), row_sem.at[p], (r, col_of(yhi, xx, core)))
            send(piece(row_vec, p), piece(row_vec, p), row_sem.at[p], (r, pair))
    phase("prodrows2")
    products(2 * UNROLL, slots, cols_s, col_split, True)
    phase("scatrows")
    place = rows_v[...]
    owner = place // 16
    scatter(
        ((owner % 2) * 8 + ((owner // 2) % 4) * 2 + owner // 8) * 16 + place % 16, part_rows
    )
    half = part_rows.shape[1] // 2

    def half_of(cc):
        return part_rows.at[:, pl.ds(pl.multiple_of(cc * half, half), half), :]

    send(half_of(1 - core), row_pair, pair_sem.at[0], (r, pair))

    phase("waitrowvec")
    for yy in (yhi, 1 - yhi):
        for xx in [x] + xs:
            p = col_of(yy, xx, 1 - core)
            arrived(piece(row_vec, p), row_sem.at[p], (r, pair))
    row_steps = list(itertools.product(range(2), range(4), range(2)))[1:]
    row_group = [(r, col_of((yhi + a) % 2, (x + b) % 4, (core + d) % 2)) for a, b, d in row_steps]
    row_back = [
        (r, col_of((yhi + a) % 2, (x + 4 - b) % 4, (core + d) % 2)) for a, b, d in row_steps
    ]
    phase("split2")
    split_vectors(row_vec, row_split)
    phase("prodcols1")
    products(0, UNROLL, rows_s, row_split, False)
    phase("waitpair")
    arrived(row_pair, pair_sem.at[0], (r, pair))
    mine = half_of(core)
    for v in range(8):
        row_pair[v] = row_pair[v] + mine[v]
    for d, xx in enumerate(xs):
        send(
            row_pair.at[:, pl.ds(pl.multiple_of(xx * 2 * count, 2 * count), 2 * count), :],
            row_ring.at[d],
            ring_sem.at[d],
            (r, col_of(yhi, xx, core)),
        )
    early_one[c] = early_send[0]
    for peer in row_group:
        send(early_send.at[0], early_one.at[c], one_sem.at[c], peer)
    phase("prodcols2")
    products(UNROLL, slots, rows_s, row_split, False)
    phase("scatcols")
    scatter(cols_v[...], part_cols)

    def lot(ref, k):
        return ref.at[:, pl.ds(pl.multiple_of(k * count, count), count), :]

    for d, zz in enumerate(zn):
        send(
            part_cols.at[:, pl.ds(pl.multiple_of(zz * 2 * count, 2 * count), 2 * count), :],
            col_near.at[d],
            back_sem.at[d],
            (row_of(zz, ylo), c),
        )
    send(lot(part_cols, far[0]), col_far.at[0], back_sem.at[2], far)
    send(
        lot(part_cols, row_of(zs[0], ylo)), col_far.at[1], back_sem.at[3], (row_of(zs[0], ylo), c)
    )

    phase("near")
    for d in range(2):
        arrived(col_near.at[d], back_sem.at[d], (row_of(zn[1 - d], ylo), c))
    at = pl.multiple_of((1 - ylo) * count, count)
    away = lot(part_cols, row_peer)
    for v in range(8):
        col_send[v] = away[v] + (col_near[0, v, pl.ds(at, count), :] + col_near[1, v, pl.ds(at, count), :])
    send(col_send, col_last, last_sem.at[1], (row_peer, c))

    phase("ringrow")
    for d in range(3):
        back = (x + (2, 3, 1)[d]) % 4
        arrived(row_ring.at[d], ring_sem.at[d], (r, col_of(yhi, back, core)))
    for v in range(8):
        own = row_pair[v, pl.ds(pl.multiple_of(x * 2 * count, 2 * count), 2 * count), :]
        row_sum[v] = (own + row_ring[0, v]) + (row_ring[1, v] + row_ring[2, v])
    send(lot(row_sum, 1 - yhi), row_last, last_sem.at[0], (r, col_peer))

    phase("waitfar")
    arrived(col_far.at[0], back_sem.at[2], far)
    arrived(col_far.at[1], back_sem.at[3], (row_of(zs[0], ylo), c))
    home = pl.multiple_of(ylo * count, count)
    row_mine, col_mine = lot(row_sum, yhi), lot(part_cols, r)
    for v in range(8):
        near = col_near[0, v, pl.ds(home, count), :] + col_near[1, v, pl.ds(home, count), :]
        total = (row_mine[v] + col_mine[v]) + (col_far[0, v] + col_far[1, v])
        image[v * count : (v + 1) * count, :] = total + near
    phase("early1")
    for peer in row_back:
        arrived(early_one.at[peer[1]], one_sem.at[peer[1]], peer)
    total = early_one[0]
    for i in range(1, early_one.shape[0]):
        total = total + early_one[i]
    early_send[1] = total
    early_two[r] = total
    for peer in col_group:
        send(early_send.at[1], early_two.at[r], two_sem.at[r], peer)
    phase("waitlast")
    arrived(col_last, last_sem.at[1], (row_peer, c))
    arrived(row_last, last_sem.at[0], (r, col_peer))
    phase("shifted")
    for v in range(8):
        part = slice(v * count, (v + 1) * count)
        image[part, :] = image[part, :] + (row_last[v] + col_last[v])
    for t in range(count):
        at = slice(t * 128, (t + 1) * 128)
        shifted[:, at] = image[pl.ds(t, 8, stride=count), :] + (diag[t : t + 1, :] - SHIFT) * now[:, at]
    shifted_copy = pltpu.make_async_copy(shifted, shifted_out, in_sem.at[0])
    shifted_copy.start()

    phase("gram")
    value = shifted[...]
    gram = dot_exact(value, jnp.concatenate([value, lanczos[...]], axis=0), NT_DIMS)
    place, lane = iota((24, 256), 0), iota((24, 256), 1)
    spread = ((lane // 64 == place // 8) & (lane % 8 == place % 8)).astype(F32)
    flat = dot_exact(gram, spread, NN_DIMS)
    flat = jnp.where((iota((8, 256), 1) // 8) % 8 == iota((8, 256), 0), flat, 0.0)
    flat = jnp.sum(flat, axis=0, keepdims=True)
    final_send[0:1, :] = flat[:, 0:128]
    final_send[1:2, :] = flat[:, 128:256]
    phase("final")
    me = r * early_one.shape[0] + c
    own_copy = pltpu.make_async_copy(final_send, final_all.at[me], in_sem.at[2])
    own_copy.start()
    steps = sorted(
        itertools.product(range(4), range(2), range(2), range(4), range(2)),
        key=lambda s: -(min(s[0], 4 - s[0]) + s[1] + 2 * s[2] + min(s[3], 4 - s[3])),
    )
    steps.remove((0, 0, 0, 0, 0))
    lasts = []
    for a, b, d, e, f in steps:
        peer = (
            row_of((z + a) % 4, (ylo + b) % 2),
            col_of((yhi + d) % 2, (x + e) % 4, (core + f) % 2),
        )
        copy = pltpu.make_async_remote_copy(
            src_ref=final_send,
            dst_ref=final_all.at[me],
            send_sem=all_sem.at[0],
            recv_sem=all_sem.at[1],
            device_id=peer,
            device_id_type=MESH,
        )
        copy.start()
        lasts.append(peer)
    phase("early2")
    for peer in col_back:
        arrived(early_two.at[peer[0]], two_sem.at[peer[0]], peer)
    total = early_two[0]
    for i in range(1, early_two.shape[0]):
        total = total + early_two[i]
    early_send[2] = total
    early_copy = pltpu.make_async_copy(early_send.at[2], early_out, in_sem.at[1])
    early_copy.start()

    phase("waitfinal")
    own_copy.wait()
    others = final_all.at[0 : len(steps)]
    waiter = pltpu.make_async_remote_copy(
        src_ref=others,
        dst_ref=others,
        send_sem=all_sem.at[0],
        recv_sem=all_sem.at[1],
        device_id=lasts[0],
        device_id_type=MESH,
    )
    waiter.wait_recv()
    phase("sum")
    final_sum[...] = jnp.sum(final_all[...], axis=0)
    final_copy = pltpu.make_async_copy(final_sum, final_out, in_sem.at[2])
    final_copy.start()
    phase("waitsends")
    for copy in sends:
        copy.wait_send()
    waiter.wait_send()
    shifted_copy.wait()
    early_copy.wait()
    final_copy.wait()
    phase(None)


def finish(scale, shifted, early, final, now, prev, coupling, next_out, alpha_out, beta_out):
    line, lane = iota((8, 16), 0), iota((8, 16), 1)
    flat = jnp.concatenate([final[0:1, :], final[1:2, :]], axis=1) * scale
    flat = jnp.where((iota((8, 256), 1) // 8) % 8 == iota((8, 256), 0), flat, 0.0)
    high = flat.astype(BF16)
    rest = flat - high.astype(F32)
    mid = rest.astype(BF16)
    low = (rest - mid.astype(F32)).astype(BF16)
    parts = jnp.concatenate([high.astype(F32), mid.astype(F32), low.astype(F32)], axis=0).astype(BF16)
    place, at = iota((16, 256), 0), iota((16, 256), 1)

    def gathered(block):
        pick = ((at // 64 == block) & (at % 8 == place % 8)).astype(F32).astype(BF16)
        out = lax.dot_general(parts, pick, NT_DIMS, preferred_element_type=F32)
        return (out[0:8] + out[8:16]) + out[16:24]

    cross = gathered(1 + place // 8)
    square = gathered(jnp.where(place < 8, 0, -1))
    known = early[:, 0:16] * scale
    eye = (line == lane).astype(F32)
    shift_eye = (line + 8 == lane).astype(F32)
    coupled = dot_exact(coupling[...], shift_eye, NN_DIMS)
    alpha_t = cross + SHIFT * known[0:8]
    weights = jnp.where(lane < 8, SHIFT * eye - alpha_t, -coupled)
    zeros = jnp.zeros((8, 16), F32)
    mixed = cross + 0.5 * dot_exact(weights, known, NN_DIMS)
    once = dot_exact(mixed, jnp.concatenate([weights, zeros], axis=0), NT_DIMS)
    again = dot_exact(weights, jnp.concatenate([mixed, zeros], axis=0), NT_DIMS)
    residual = shifted[...] + dot_exact(
        weights, jnp.concatenate([now[...], prev[...]], axis=0), NN_DIMS
    )
    work = (square + (once + again)) + shift_eye
    for j in range(8):
        lead = jnp.broadcast_to(work[j : j + 1, :], (8, 16))
        column = jnp.broadcast_to(work[:, j : j + 1], (8, 16))
        pivot = jnp.broadcast_to(work[j : j + 1, j : j + 1], (8, 16))
        work = jnp.where(line > j, work - (column / pivot) * lead, work)
    pivots = jnp.sum(jnp.where(line == lane, work, 0.0), axis=1, keepdims=True)
    work = work / jnp.sqrt(pivots)
    next_out[...] = dot_exact(work[:, 8:16], residual, NN_DIMS)
    beta_out[...] = jnp.where(line <= lane, work, 0.0)[:, 0:8]
    alpha_out[...] = dot_exact(eye[:, 0:8], alpha_t[:, 0:8], NT_DIMS)


def local(tiles, tile_rows, tile_cols, tile_counts, block_now, block_prev, coupling, diag_energy):
    slots, tile_width = tiles.shape[2], tiles.shape[3]
    vectors, width = block_now.shape
    n_row, n_col = lax.axis_size("row"), lax.axis_size("col")
    count = width // tile_width
    rows, cols = tile_rows.reshape(1, slots), tile_cols.reshape(1, slots)
    hbm = pl.BlockSpec(memory_space=pltpu.HBM)
    vmem = pl.BlockSpec(memory_space=pltpu.VMEM)
    dma = pltpu.SemaphoreType.DMA
    n_rt, n_ct = n_col * count, n_row * count
    shape = jax.ShapeDtypeStruct
    shifted, early, final = pl.pallas_call(
        kernel,
        out_shape=(shape((vectors, width), F32), shape((16, 128), F32), shape((2, 128), F32)),
        in_specs=[hbm] * 9,
        out_specs=(hbm, hbm, hbm),
        scratch_shapes=[
            pltpu.VMEM((slots, tile_width, tile_width), F32),
            pltpu.VMEM((slots, tile_width, tile_width), BF16),
            pltpu.VMEM((slots, tile_width, tile_width), BF16),
            pltpu.SMEM((slots,), jnp.int32),
            pltpu.SMEM((slots,), jnp.int32),
            pltpu.SMEM((1, 1), jnp.int32),
            pltpu.VMEM((1, slots), jnp.int32),
            pltpu.VMEM((1, slots), jnp.int32),
            pltpu.VMEM((2 * vectors, width), F32),
            pltpu.VMEM((count, tile_width), F32),
            pltpu.VMEM((vectors, n_row * width), F32),
            pltpu.VMEM((vectors, n_col * width), F32),
            pltpu.VMEM((n_ct, 16, tile_width), BF16),
            pltpu.VMEM((n_rt, 16, tile_width), BF16),
            pltpu.VMEM((vectors * slots, tile_width), F32),
            pltpu.VMEM((vectors, n_rt, tile_width), F32),
            pltpu.VMEM((vectors, n_ct, tile_width), F32),
            pltpu.VMEM((vectors, n_rt // 2, tile_width), F32),
            pltpu.VMEM((3, vectors, 2 * count, tile_width), F32),
            pltpu.VMEM((vectors, 2 * count, tile_width), F32),
            pltpu.VMEM((vectors, count, tile_width), F32),
            pltpu.VMEM((2, vectors, 2 * count, tile_width), F32),
            pltpu.VMEM((2, vectors, count, tile_width), F32),
            pltpu.VMEM((vectors, count, tile_width), F32),
            pltpu.VMEM((vectors, count, tile_width), F32),
            pltpu.VMEM((vectors * count, tile_width), F32),
            pltpu.VMEM((vectors, width), F32),
            pltpu.VMEM((3, 16, 128), F32),
            pltpu.VMEM((n_col, 16, 128), F32),
            pltpu.VMEM((n_row, 16, 128), F32),
            pltpu.VMEM((2, 128), F32),
            pltpu.VMEM((n_row * n_col, 2, 128), F32),
            pltpu.VMEM((2, 128), F32),
            dma((slots // CHUNK,)),
            dma((8,)),
            dma((64,)),
            dma((n_row,)),
            dma((n_col,)),
            dma((1,)),
            dma((3,)),
            dma((2,)),
            dma((4,)),
            dma((n_col,)),
            dma((n_row,)),
            dma((2,)),
        ],
        compiler_params=pltpu.CompilerParams(
            collective_id=0, has_side_effects=True, vmem_limit_bytes=54 * 2**20
        ),
    )(
        tiles.reshape(slots, tile_width, tile_width),
        rows.reshape(slots),
        cols.reshape(slots),
        tile_counts,
        rows,
        cols,
        block_now,
        block_prev,
        diag_energy.reshape(count, tile_width),
    )
    return pl.pallas_call(
        functools.partial(finish, 1.0 / (width * n_row * n_col)),
        out_shape=(shape((vectors, width), F32), shape((8, 8), F32), shape((8, 8), F32)),
        in_specs=[vmem] * 6,
        out_specs=(vmem, vmem, vmem),
    )(shifted, early, final, block_now, block_prev, coupling)


def solution(mesh):
    return jax.shard_map(
        local,
        mesh=mesh,
        in_specs=(
            P("row", "col", None, None, None),
            P("row", "col", None),
            P("row", "col", None),
            P("row", "col"),
            P(None, ("row", "col")),
            P(None, ("row", "col")),
            P(),
            P(("row", "col")),
        ),
        out_specs=(P(None, ("row", "col")), P(), P()),
        check_vma=False,
    )
```

time: 66.9 us -> 51.4 us (0.77)
  Pallas kernels: 61.3 us -> 49.9 us
  local copies, waits for them, and re-layouts: 4.02 us -> 0 us
    pallas_call x1 -> x2, Pallas kernels: 61.3 us -> 49.9 us  [the longest x1 46.7 us: local(): pl.pallas_call(kernel, out_shape=(shape((vectors, width), F32), shape((16...]
    unnamed x3 -> x0, local copies, waits for them, and re-layouts: 4.02 us -> none
where the time goes in v2:
time: 51.4 us; the launch traced here: 51.2 us
  Pallas kernels  49.9 us (97%)
  between operations  1.29 us (3%)
    pallas_call x1, Pallas kernels, local(): pl.pallas_call(kernel, out_shape=(shape((vectors, width), F32), shape((16...  46.7 us
    pallas_call x1, Pallas kernels, local(): pl.pallas_call(functools.partial(finish, 1.0 / (width * n_row * n_col)),...  3.25 us

profile of v2, /device:TPU:1, one launch (start us, length us, event | category | flops | bytes accessed | tf_op | source)
XLA Modules:
  0.0 51.2 jit_solution(6504674568677848657)
XLA Ops:
  1.3 46.7 %shard_map.103 = (f32[8,2048]{1,0:T(8,128)}, f32[16,128]{1,0:T(8,128)}, f32[2,128]{1,0:T(2,128)}) custom-call(f32[256,128,128]{2,1,0:T(8,128)} %bitcast.6, s32[256]{0:T(256)} %bitcast.8, s32[256]{0:T(256)} %bitcast.10, s32[1,1]{1,0:T(1,128)S(6)} %copy.11.count_h, s32[1,256]{1,0:T(1,128)} %bitcast.9, s32[1,256]{1,0:T(1,128)} %bitcast.11, f32[8,2048]{1,0:T(8,128)} %now.1, ...), custom_call_target="tpu_custom_call" | custom-call | tf_op jit(solution)/shard_map/pallas_call | solution.py:544
  48.0 3.3 %shard_map.104 = (f32[8,2048]{1,0:T(8,128)}, f32[8,8]{1,0:T(8,128)}, f32[8,8]{1,0:T(8,128)}) custom-call(f32[8,2048]{1,0:T(8,128)} %get-tuple-element.6.shifted, f32[16,128]{1,0:T(8,128)} %get-tuple-element.7.early, f32[2,128]{1,0:T(2,128)} %get-tuple-element.8.final, f32[8,2048]{1,0:T(8,128)} %now.1, f32[8,2048]{1,0:T(8,128)} %prev.1, f32[8,8]{1,0:T(8,128)} %coupling.1), custom_call_target="tpu_custom_call" | custom-call | tf_op jit(solution)/shard_map/pallas_call | solution.py:610

commit v3 on v2

--- a/solution.py
+++ b/solution.py
@@ -63,8 +63,9 @@
     part_rows,
     part_cols,
     row_pair,
-    row_ring,
-    row_sum,
+    row_near,
+    row_far,
+    row_send,
     row_last,
     col_near,
     col_far,
@@ -118,7 +119,8 @@
     row_peer = row_of(z, 1 - ylo)
     col_peer = col_of(1 - yhi, x, core)
     pair = col_of(yhi, x, 1 - core)
-    zn = zs[1:]
+    zn, xn = zs[1:], xs[1:]
+    across = (r, col_of(1 - yhi, xs[0], core))
     far = (row_of(zs[0], 1 - ylo), c)
     col_steps = [(2, 1), (1, 1), (3, 1), (2, 0), (0, 1), (1, 0), (3, 0)]
     col_group = [(row_of((z + a) % 4, (ylo + b) % 2), c) for a, b in col_steps]
@@ -127,7 +129,7 @@
     phase("start")
     barrier = pltpu.get_barrier_semaphore()
     first_peers = [(row_peer, c), (r, col_peer), far] + [(row_of(zz, ylo), c) for zz in zs]
-    first_peers += [(r, col_of(yhi, xx, core)) for xx in xs] + [(r, pair)]
+    first_peers += [(r, col_of(yhi, xx, core)) for xx in xs] + [(r, pair), across]
     for peer in first_peers:
         pl.semaphore_signal(barrier, inc=1, device_id=peer, device_id_type=MESH)
 
@@ -166,12 +168,13 @@
     pl.semaphore_wait(barrier, len(first_peers))
 
     sends = []
+    numbers = itertools.count()
 
     def send(src, dst, recv, peer):
         copy = pltpu.make_async_remote_copy(
             src_ref=src,
             dst_ref=dst,
-            send_sem=send_sem.at[len(sends)],
+            send_sem=send_sem.at[next(numbers)],
             recv_sem=recv,
             device_id=peer,
             device_id_type=MESH,
@@ -335,10 +338,10 @@
     mine = half_of(core)
     for v in range(8):
         row_pair[v] = row_pair[v] + mine[v]
-    for d, xx in enumerate(xs):
+    for d, xx in enumerate(xn):
         send(
             row_pair.at[:, pl.ds(pl.multiple_of(xx * 2 * count, 2 * count), 2 * count), :],
-            row_ring.at[d],
+            row_near.at[d],
             ring_sem.at[d],
             (r, col_of(yhi, xx, core)),
         )
@@ -346,7 +349,18 @@
     for peer in row_group:
         send(early_send.at[0], early_one.at[c], one_sem.at[c], peer)
     phase("prodcols2")
-    products(UNROLL, slots, rows_s, row_split, False)
+    products(UNROLL, 3 * UNROLL, rows_s, row_split, False)
+    phase("rowfar")
+    opposite = xs[0] * 2 * count
+    for d, (yy, peer) in enumerate([(1 - yhi, across), (yhi, (r, col_of(yhi, xs[0], core)))]):
+        send(
+            row_pair.at[:, pl.ds(pl.multiple_of(opposite + yy * count, count), count), :],
+            row_far.at[d],
+            ring_sem.at[2 + d],
+            peer,
+        )
+    phase("prodcols3")
+    products(3 * UNROLL, slots, rows_s, row_split, False)
     phase("scatcols")
     scatter(cols_v[...], part_cols)
 
@@ -360,11 +374,20 @@
             back_sem.at[d],
             (row_of(zz, ylo), c),
         )
+    phase("rownear")
+    for d in range(2):
+        arrived(row_near.at[d], ring_sem.at[d], (r, col_of(yhi, xn[1 - d], core)))
+    mine_at = pl.multiple_of(x * 2 * count + yhi * count, count)
+    away_at = pl.multiple_of(x * 2 * count + (1 - yhi) * count, count)
+    for v in range(8):
+        at = pl.ds(pl.multiple_of((1 - yhi) * count, count), count)
+        row_send[v] = row_pair[v, pl.ds(away_at, count), :] + (row_near[0, v, at, :] + row_near[1, v, at, :])
+    send(row_send, row_last, last_sem.at[0], (r, col_peer))
+    phase("colfar")
     send(lot(part_cols, far[0]), col_far.at[0], back_sem.at[2], far)
     send(
         lot(part_cols, row_of(zs[0], ylo)), col_far.at[1], back_sem.at[3], (row_of(zs[0], ylo), c)
     )
-
     phase("near")
     for d in range(2):
         arrived(col_near.at[d], back_sem.at[d], (row_of(zn[1 - d], ylo), c))
@@ -374,24 +397,19 @@
         col_send[v] = away[v] + (col_near[0, v, pl.ds(at, count), :] + col_near[1, v, pl.ds(at, count), :])
     send(col_send, col_last, last_sem.at[1], (row_peer, c))
 
-    phase("ringrow")
-    for d in range(3):
-        back = (x + (2, 3, 1)[d]) % 4
-        arrived(row_ring.at[d], ring_sem.at[d], (r, col_of(yhi, back, core)))
-    for v in range(8):
-        own = row_pair[v, pl.ds(pl.multiple_of(x * 2 * count, 2 * count), 2 * count), :]
-        row_sum[v] = (own + row_ring[0, v]) + (row_ring[1, v] + row_ring[2, v])
-    send(lot(row_sum, 1 - yhi), row_last, last_sem.at[0], (r, col_peer))
-
     phase("waitfar")
+    arrived(row_far.at[0], ring_sem.at[2], across)
+    arrived(row_far.at[1], ring_sem.at[3], (r, col_of(yhi, xs[0], core)))
     arrived(col_far.at[0], back_sem.at[2], far)
     arrived(col_far.at[1], back_sem.at[3], (row_of(zs[0], ylo), c))
-    home = pl.multiple_of(ylo * count, count)
-    row_mine, col_mine = lot(row_sum, yhi), lot(part_cols, r)
+    home = pl.ds(pl.multiple_of(ylo * count, count), count)
+    own = pl.ds(pl.multiple_of(yhi * count, count), count)
+    col_mine = lot(part_cols, r)
     for v in range(8):
-        near = col_near[0, v, pl.ds(home, count), :] + col_near[1, v, pl.ds(home, count), :]
-        total = (row_mine[v] + col_mine[v]) + (col_far[0, v] + col_far[1, v])
-        image[v * count : (v + 1) * count, :] = total + near
+        total = (row_pair[v, pl.ds(mine_at, count), :] + col_mine[v]) + (col_far[0, v] + col_far[1, v])
+        total = total + (row_far[0, v] + row_far[1, v])
+        total = total + (row_near[0, v, own, :] + row_near[1, v, own, :])
+        image[v * count : (v + 1) * count, :] = total + (col_near[0, v, home, :] + col_near[1, v, home, :])
     phase("early1")
     for peer in row_back:
         arrived(early_one.at[peer[1]], one_sem.at[peer[1]], peer)
@@ -487,6 +505,16 @@
 
 
 def finish(scale, shifted, early, final, now, prev, coupling, next_out, alpha_out, beta_out):
+    open_scope = []
+
+    def phase(name):
+        if open_scope:
+            open_scope.pop().__exit__(None, None, None)
+        if name:
+            open_scope.append(jax.named_scope(name))
+            open_scope[0].__enter__()
+
+    phase("Bgram")
     line, lane = iota((8, 16), 0), iota((8, 16), 1)
     flat = jnp.concatenate([final[0:1, :], final[1:2, :]], axis=1) * scale
     flat = jnp.where((iota((8, 256), 1) // 8) % 8 == iota((8, 256), 0), flat, 0.0)
@@ -517,17 +545,40 @@
     residual = shifted[...] + dot_exact(
         weights, jnp.concatenate([now[...], prev[...]], axis=0), NN_DIMS
     )
-    work = (square + (once + again)) + shift_eye
-    for j in range(8):
-        lead = jnp.broadcast_to(work[j : j + 1, :], (8, 16))
-        column = jnp.broadcast_to(work[:, j : j + 1], (8, 16))
-        pivot = jnp.broadcast_to(work[j : j + 1, j : j + 1], (8, 16))
-        work = jnp.where(line > j, work - (column / pivot) * lead, work)
-    pivots = jnp.sum(jnp.where(line == lane, work, 0.0), axis=1, keepdims=True)
-    work = work / jnp.sqrt(pivots)
-    next_out[...] = dot_exact(work[:, 8:16], residual, NN_DIMS)
-    beta_out[...] = jnp.where(line <= lane, work, 0.0)[:, 0:8]
+    phase("Bchol")
+    gram = square + (once + again)
+
+    def entry(a, b):
+        return jnp.broadcast_to(gram[a : a + 1, b : b + 1], (8, 128))
+
+    upper = {(a, b): entry(a, b) for a in range(8) for b in range(a, 8)}
+    inverse = {}
+    for a in range(8):
+        pivot = 1.0 / upper[a, a]
+        for b in range(a + 1, 8):
+            factor = upper[a, b] * pivot
+            for k in range(b, 8):
+                upper[b, k] = upper[b, k] - factor * upper[a, k]
+            for k in range(a):
+                inverse[b, k] = inverse[b, k] - factor * inverse[a, k]
+            inverse[b, a] = -factor
+    line, lane = iota((8, 128), 0), iota((8, 128), 1)
+    solve = jnp.zeros((8, 128), F32)
+    beta = jnp.zeros((8, 128), F32)
+    for a in range(8):
+        root = jnp.sqrt(upper[a, a])
+        scale_row = 1.0 / root
+        solve = jnp.where((line == a) & (lane == a), scale_row, solve)
+        beta = jnp.where((line == a) & (lane == a), root, beta)
+        for k in range(a):
+            solve = jnp.where((line == a) & (lane == k), inverse[a, k] * scale_row, solve)
+        for b in range(a + 1, 8):
+            beta = jnp.where((line == a) & (lane == b), upper[a, b] * scale_row, beta)
+    phase("Bsolve")
+    next_out[...] = dot_exact(solve[:, 0:8], residual, NN_DIMS)
+    beta_out[...] = beta[:, 0:8]
     alpha_out[...] = dot_exact(eye[:, 0:8], alpha_t[:, 0:8], NT_DIMS)
+    phase(None)
 
 
 def local(tiles, tile_rows, tile_cols, tile_counts, block_now, block_prev, coupling, diag_energy):
@@ -565,8 +616,9 @@
             pltpu.VMEM((vectors, n_rt, tile_width), F32),
             pltpu.VMEM((vectors, n_ct, tile_width), F32),
             pltpu.VMEM((vectors, n_rt // 2, tile_width), F32),
-            pltpu.VMEM((3, vectors, 2 * count, tile_width), F32),
-            pltpu.VMEM((vectors, 2 * count, tile_width), F32),
+            pltpu.VMEM((2, vectors, 2 * count, tile_width), F32),
+            pltpu.VMEM((2, vectors, count, tile_width), F32),
+            pltpu.VMEM((vectors, count, tile_width), F32),
             pltpu.VMEM((vectors, count, tile_width), F32),
             pltpu.VMEM((2, vectors, 2 * count, tile_width), F32),
             pltpu.VMEM((2, vectors, count, tile_width), F32),
@@ -586,7 +638,7 @@
             dma((n_row,)),
             dma((n_col,)),
             dma((1,)),
-            dma((3,)),
+            dma((4,)),
             dma((2,)),
             dma((4,)),
             dma((n_col,)),

time: 51.4 us -> 49.7 us (0.967)
  Pallas kernels: 49.9 us -> 48.2 us
    pallas_call x1, Pallas kernels: 46.7 us -> 45.6 us  [local(): pl.pallas_call(kernel, out_shape=(shape((vectors, width), F32), shape((16...]
    pallas_call x1, Pallas kernels: 3.25 us -> 2.56 us  [local(): pl.pallas_call(functools.partial(finish, 1.0 / (width * n_row * n_col)),...]
where the time goes in v3:
time: 49.7 us; the launch traced here: 49.5 us
  Pallas kernels  48.2 us (97%)
  between operations  1.29 us (3%)
    pallas_call x1, Pallas kernels, local(): pl.pallas_call(kernel, out_shape=(shape((vectors, width), F32), shape((16...  45.6 us
    pallas_call x1, Pallas kernels, local(): pl.pallas_call(functools.partial(finish, 1.0 / (width * n_row * n_col)),...  2.56 us

profile of v3, /device:TPU:1, one launch (start us, length us, event | category | flops | bytes accessed | tf_op | source)
XLA Modules:
  0.0 49.5 jit_solution(1413946000950966546)
XLA Ops:
  1.3 45.6 %shard_map.103 = (f32[8,2048]{1,0:T(8,128)}, f32[16,128]{1,0:T(8,128)}, f32[2,128]{1,0:T(2,128)}) custom-call(f32[256,128,128]{2,1,0:T(8,128)} %bitcast.6, s32[256]{0:T(256)} %bitcast.8, s32[256]{0:T(256)} %bitcast.10, s32[1,1]{1,0:T(1,128)S(6)} %copy.11.count_h, s32[1,256]{1,0:T(1,128)} %bitcast.9, s32[1,256]{1,0:T(1,128)} %bitcast.11, f32[8,2048]{1,0:T(8,128)} %now.1, ...), custom_call_target="tpu_custom_call" | custom-call | tf_op jit(solution)/shard_map/pallas_call | solution.py:595
  46.9 2.6 %shard_map.104 = (f32[8,2048]{1,0:T(8,128)}, f32[8,8]{1,0:T(8,128)}, f32[8,8]{1,0:T(8,128)}) custom-call(f32[8,2048]{1,0:T(8,128)} %get-tuple-element.6.shifted, f32[16,128]{1,0:T(8,128)} %get-tuple-element.7.early, f32[2,128]{1,0:T(2,128)} %get-tuple-element.8.final, f32[8,2048]{1,0:T(8,128)} %now.1, f32[8,2048]{1,0:T(8,128)} %prev.1, f32[8,8]{1,0:T(8,128)} %coupling.1), custom_call_target="tpu_custom_call" | custom-call | tf_op jit(solution)/shard_map/pallas_call | solution.py:662

commit v4 on v3

--- a/solution.py
+++ b/solution.py
@@ -26,6 +26,12 @@
 def split_rows(value):
     high = value.astype(BF16).astype(F32)
     return jnp.concatenate([high, value - high], axis=0).astype(BF16)
+
+
+def three_parts(value):
+    high = value.astype(BF16).astype(F32)
+    mid = (value - high).astype(BF16).astype(F32)
+    return jnp.concatenate([high, mid, (value - high) - mid], axis=0).astype(BF16)
 
 
 def iota(shape, axis):
@@ -42,7 +48,7 @@
     now_h,
     prev_h,
     diag_h,
-    shifted_out,
+    shifted,
     early_out,
     final_out,
     tile_f32,
@@ -72,13 +78,12 @@
     col_send,
     col_last,
     image,
-    shifted,
     early_send,
     early_one,
     early_two,
     final_send,
     final_all,
-    final_sum,
+    known_split,
     tile_sem,
     in_sem,
     send_sem,
@@ -245,6 +250,9 @@
     phase("early")
     early_send[...] = jnp.zeros_like(early_send)
     known = lanczos[...]
+    high = known.astype(BF16)
+    known_split[0] = high
+    known_split[1] = (known - high.astype(F32)).astype(BF16)
     early_send[0, :, 0:16] = dot_exact(known, known, NT_DIMS)
 
     phase("waitcolvec")
@@ -266,21 +274,16 @@
     split_vectors(col_vec, col_split)
 
     def products(first, last, index, vectors, transposed):
-        def body(g, _):
-            for u in range(UNROLL):
-                m = g * UNROLL + u
-                left = vectors[index[m]]
-                if transposed:
-                    weights = jnp.concatenate([tile_hi[m], tile_lo[m]], axis=0)
-                    out = lax.dot_general(left, weights, NT_DIMS, preferred_element_type=F32)
-                else:
-                    weights = jnp.concatenate([tile_hi[m], tile_lo[m]], axis=1)
-                    out = lax.dot_general(left, weights, NN_DIMS, preferred_element_type=F32)
-                total = (out[0:8, 0:128] + out[8:16, 0:128]) + out[0:8, 128:256]
-                images[pl.ds(m, 8, stride=slots), :] = total
-            return 0
-
-        lax.fori_loop(first // UNROLL, last // UNROLL, body, 0)
+        for m in range(first, last):
+            left = vectors[index[m]]
+            if transposed:
+                weights = jnp.concatenate([tile_hi[m], tile_lo[m]], axis=0)
+                out = lax.dot_general(left, weights, NT_DIMS, preferred_element_type=F32)
+            else:
+                weights = jnp.concatenate([tile_hi[m], tile_lo[m]], axis=1)
+                out = lax.dot_general(left, weights, NN_DIMS, preferred_element_type=F32)
+            total = (out[0:8, 0:128] + out[8:16, 0:128]) + out[0:8, 128:256]
+            images[pl.ds(m, 8, stride=slots), :] = total
 
     used = iota((1, slots), 1) < count_s[0, 0]
 
@@ -430,15 +433,21 @@
     for t in range(count):
         at = slice(t * 128, (t + 1) * 128)
         shifted[:, at] = image[pl.ds(t, 8, stride=count), :] + (diag[t : t + 1, :] - SHIFT) * now[:, at]
-    shifted_copy = pltpu.make_async_copy(shifted, shifted_out, in_sem.at[0])
-    shifted_copy.start()
 
     phase("gram")
-    value = shifted[...]
-    gram = dot_exact(value, jnp.concatenate([value, lanczos[...]], axis=0), NT_DIMS)
-    place, lane = iota((24, 256), 0), iota((24, 256), 1)
-    spread = ((lane // 64 == place // 8) & (lane % 8 == place % 8)).astype(F32)
-    flat = dot_exact(gram, spread, NN_DIMS)
+    halves = split_rows(shifted[...])
+    gram = lax.dot_general(
+        halves,
+        jnp.concatenate([halves, known_split[0], known_split[1]], axis=0),
+        NT_DIMS,
+        preferred_element_type=F32,
+    )
+    gram = gram[0:8] + gram[8:16]
+    place, lane = iota((48, 256), 0), iota((48, 256), 1)
+    block = jnp.where(place < 16, 0, 1 + (place // 8) % 2)
+    spread = ((lane // 64 == block) & (lane % 8 == place % 8)).astype(F32).astype(BF16)
+    flat = lax.dot_general(three_parts(gram), spread, NN_DIMS, preferred_element_type=F32)
+    flat = (flat[0:8] + flat[8:16]) + flat[16:24]
     flat = jnp.where((iota((8, 256), 1) // 8) % 8 == iota((8, 256), 0), flat, 0.0)
     flat = jnp.sum(flat, axis=0, keepdims=True)
     final_send[0:1, :] = flat[:, 0:128]
@@ -474,9 +483,7 @@
     total = early_two[0]
     for i in range(1, early_two.shape[0]):
         total = total + early_two[i]
-    early_send[2] = total
-    early_copy = pltpu.make_async_copy(early_send.at[2], early_out, in_sem.at[1])
-    early_copy.start()
+    early_out[...] = total
 
     phase("waitfinal")
     own_copy.wait()
@@ -491,16 +498,11 @@
     )
     waiter.wait_recv()
     phase("sum")
-    final_sum[...] = jnp.sum(final_all[...], axis=0)
-    final_copy = pltpu.make_async_copy(final_sum, final_out, in_sem.at[2])
-    final_copy.start()
+    final_out[...] = jnp.sum(final_all[...], axis=0)
     phase("waitsends")
     for copy in sends:
         copy.wait_send()
     waiter.wait_send()
-    shifted_copy.wait()
-    early_copy.wait()
-    final_copy.wait()
     phase(None)
 
 
@@ -518,11 +520,7 @@
     line, lane = iota((8, 16), 0), iota((8, 16), 1)
     flat = jnp.concatenate([final[0:1, :], final[1:2, :]], axis=1) * scale
     flat = jnp.where((iota((8, 256), 1) // 8) % 8 == iota((8, 256), 0), flat, 0.0)
-    high = flat.astype(BF16)
-    rest = flat - high.astype(F32)
-    mid = rest.astype(BF16)
-    low = (rest - mid.astype(F32)).astype(BF16)
-    parts = jnp.concatenate([high.astype(F32), mid.astype(F32), low.astype(F32)], axis=0).astype(BF16)
+    parts = three_parts(flat)
     place, at = iota((16, 256), 0), iota((16, 256), 1)
 
     def gathered(block):
@@ -596,7 +594,7 @@
         kernel,
         out_shape=(shape((vectors, width), F32), shape((16, 128), F32), shape((2, 128), F32)),
         in_specs=[hbm] * 9,
-        out_specs=(hbm, hbm, hbm),
+        out_specs=(vmem, vmem, vmem),
         scratch_shapes=[
             pltpu.VMEM((slots, tile_width, tile_width), F32),
             pltpu.VMEM((slots, tile_width, tile_width), BF16),
@@ -625,13 +623,12 @@
             pltpu.VMEM((vectors, count, tile_width), F32),
             pltpu.VMEM((vectors, count, tile_width), F32),
             pltpu.VMEM((vectors * count, tile_width), F32),
-            pltpu.VMEM((vectors, width), F32),
-            pltpu.VMEM((3, 16, 128), F32),
+            pltpu.VMEM((2, 16, 128), F32),
             pltpu.VMEM((n_col, 16, 128), F32),
             pltpu.VMEM((n_row, 16, 128), F32),
             pltpu.VMEM((2, 128), F32),
             pltpu.VMEM((n_row * n_col, 2, 128), F32),
-            pltpu.VMEM((2, 128), F32),
+            pltpu.VMEM((2, 16, width), BF16),
             dma((slots // CHUNK,)),
             dma((8,)),
             dma((64,)),
@@ -646,24 +643,30 @@
             dma((2,)),
         ],
         compiler_params=pltpu.CompilerParams(
-            collective_id=0, has_side_effects=True, vmem_limit_bytes=54 * 2**20
+            collective_id=0, has_side_effects=True, vmem_limit_bytes=52 * 2**20
         ),
     )(
-        tiles.reshape(slots, tile_width, tile_width),
-        rows.reshape(slots),
-        cols.reshape(slots),
-        tile_counts,
-        rows,
-        cols,
-        block_now,
-        block_prev,
-        diag_energy.reshape(count, tile_width),
+        *(
+            value if value is tile_counts else pltpu.with_memory_space_constraint(value, pltpu.HBM)
+            for value in (
+                tiles.reshape(slots, tile_width, tile_width),
+                rows.reshape(slots),
+                cols.reshape(slots),
+                tile_counts,
+                rows,
+                cols,
+                block_now,
+                block_prev,
+                diag_energy.reshape(count, tile_width),
+            )
+        )
     )
     return pl.pallas_call(
         functools.partial(finish, 1.0 / (width * n_row * n_col)),
         out_shape=(shape((vectors, width), F32), shape((8, 8), F32), shape((8, 8), F32)),
         in_specs=[vmem] * 6,
         out_specs=(vmem, vmem, vmem),
+        compiler_params=pltpu.CompilerParams(vmem_limit_bytes=4 * 2**20),
     )(shifted, early, final, block_now, block_prev, coupling)
 
 

time: 49.7 us -> 48.1 us (0.968)
  Pallas kernels: 48.2 us -> 46.5 us
    pallas_call x1, Pallas kernels: 2.56 us -> 1.63 us  [local(): pl.pallas_call(functools.partial(finish, 1.0 / (width * n_row * n_col)),...]
    pallas_call x1, Pallas kernels: 45.6 us -> 44.9 us  [local(): pl.pallas_call(kernel, out_shape=(shape((vectors, width), F32), shape((16...]
where the time goes in v4:
time: 48.1 us; the launch traced here: 47.9 us
  Pallas kernels  46.5 us (97%)
  between operations  1.37 us (3%)
    pallas_call x1, Pallas kernels, local(): pl.pallas_call(kernel, out_shape=(shape((vectors, width), F32), shape((16...  44.9 us
    pallas_call x1, Pallas kernels, local(): pl.pallas_call(functools.partial(finish, 1.0 / (width * n_row * n_col)),...  1.63 us

profile of v4, /device:TPU:1, one launch (start us, length us, event | category | flops | bytes accessed | tf_op | source)
XLA Modules:
  0.0 47.9 jit_solution(7745091964703515445)
XLA Ops:
  0.6 0.0 copy-start.1
  0.6 0.0 copy-start
  0.7 0.0 copy-start.2
  1.3 44.9 %shard_map.103 = (f32[8,2048]{1,0:T(8,128)S(1)}, f32[16,128]{1,0:T(8,128)S(1)}, f32[2,128]{1,0:T(2,128)S(1)}) custom-call(f32[256,128,128]{2,1,0:T(8,128)} %bitcast.6, s32[256]{0:T(256)} %bitcast.8, s32[256]{0:T(256)} %bitcast.10, s32[1,1]{1,0:T(1,128)S(6)} %copy.11.count_h, s32[1,256]{1,0:T(1,128)} %bitcast.9, s32[1,256]{1,0:T(1,128)} %bitcast.11, ...), custom_call_target="tpu_custom_call" | custom-call | tf_op jit(solution)/shard_map/pallas_call | solution.py:593
  46.2 0.0 copy-done.1
  46.3 0.0 copy-done
  46.3 0.0 copy-done.2
  46.3 1.6 %shard_map.104 = (f32[8,2048]{1,0:T(8,128)}, f32[8,8]{1,0:T(8,128)}, f32[8,8]{1,0:T(8,128)}) custom-call(f32[8,2048]{1,0:T(8,128)S(1)} %get-tuple-element.6.shifted, f32[16,128]{1,0:T(8,128)S(1)} %get-tuple-element.7.early, f32[2,128]{1,0:T(2,128)S(1)} %get-tuple-element.8.final, f32[8,2048]{1,0:T(8,128)S(1)} %copy-done, f32[8,2048]{1,0:T(8,128)S(1)} %copy-done.1, ...), custom_call_target="tpu_custom_call" | custom-call | tf_op jit(solution)/shard_map/pallas_call | solution.py:664
Async XLA Ops:
  0.6 45.6 %copy-start.1 = (f32[8,2048]{1,0:T(8,128)S(1)}, f32[8,2048]{1,0:T(8,128)}, u32[]{:S(2)}) copy-start(f32[8,2048]{1,0:T(8,128)} %prev.1) | copy-start | bytes 196612
  0.6 45.6 %copy-start = (f32[8,2048]{1,0:T(8,128)S(1)}, f32[8,2048]{1,0:T(8,128)}, u32[]{:S(2)}) copy-start(f32[8,2048]{1,0:T(8,128)} %now.1) | copy-start | bytes 196612
  0.7 45.6 %copy-start.2 = (f32[8,8]{1,0:T(8,128)S(1)}, f32[8,8]{1,0:T(8,128)}, u32[]{:S(2)}) copy-start(f32[8,8]{1,0:T(8,128)} %coupling.1) | copy-start | bytes 772

commit v5 on v4

--- a/solution.py
+++ b/solution.py
@@ -134,7 +134,7 @@
     phase("start")
     barrier = pltpu.get_barrier_semaphore()
     first_peers = [(row_peer, c), (r, col_peer), far] + [(row_of(zz, ylo), c) for zz in zs]
-    first_peers += [(r, col_of(yhi, xx, core)) for xx in xs] + [(r, pair), across]
+    first_peers += [(r, col_of(yhi, xx, core)) for xx in xs] + [(r, pair)]
     for peer in first_peers:
         pl.semaphore_signal(barrier, inc=1, device_id=peer, device_id_type=MESH)
 
@@ -377,6 +377,7 @@
             back_sem.at[d],
             (row_of(zz, ylo), c),
         )
+    send(lot(part_cols, far[0]), col_far.at[0], back_sem.at[2], far)
     phase("rownear")
     for d in range(2):
         arrived(row_near.at[d], ring_sem.at[d], (r, col_of(yhi, xn[1 - d], core)))
@@ -387,7 +388,6 @@
         row_send[v] = row_pair[v, pl.ds(away_at, count), :] + (row_near[0, v, at, :] + row_near[1, v, at, :])
     send(row_send, row_last, last_sem.at[0], (r, col_peer))
     phase("colfar")
-    send(lot(part_cols, far[0]), col_far.at[0], back_sem.at[2], far)
     send(
         lot(part_cols, row_of(zs[0], ylo)), col_far.at[1], back_sem.at[3], (row_of(zs[0], ylo), c)
     )

time: 48.1 us -> 46.9 us (0.975)
  Pallas kernels: 46.5 us -> 45.3 us
    pallas_call x1, Pallas kernels: 44.9 us -> 43.7 us  [local(): pl.pallas_call(kernel, out_shape=(shape((vectors, width), F32), shape((16...]
where the time goes in v5:
time: 46.9 us; the launch traced here: 46.7 us
  Pallas kernels  45.3 us (97%)
  between operations  1.37 us (3%)
    pallas_call x1, Pallas kernels, local(): pl.pallas_call(kernel, out_shape=(shape((vectors, width), F32), shape((16...  43.7 us
    pallas_call x1, Pallas kernels, local(): pl.pallas_call(functools.partial(finish, 1.0 / (width * n_row * n_col)),...  1.63 us

profile of v5, /device:TPU:1, one launch (start us, length us, event | category | flops | bytes accessed | tf_op | source)
XLA Modules:
  0.0 46.7 jit_solution(12437520395482634913)
XLA Ops:
  0.6 0.0 copy-start.1
  0.6 0.0 copy-start
  0.7 0.0 copy-start.2
  1.3 43.7 %shard_map.103 = (f32[8,2048]{1,0:T(8,128)S(1)}, f32[16,128]{1,0:T(8,128)S(1)}, f32[2,128]{1,0:T(2,128)S(1)}) custom-call(f32[256,128,128]{2,1,0:T(8,128)} %bitcast.6, s32[256]{0:T(256)} %bitcast.8, s32[256]{0:T(256)} %bitcast.10, s32[1,1]{1,0:T(1,128)S(6)} %copy.11.count_h, s32[1,256]{1,0:T(1,128)} %bitcast.9, s32[1,256]{1,0:T(1,128)} %bitcast.11, ...), custom_call_target="tpu_custom_call" | custom-call | tf_op jit(solution)/shard_map/pallas_call | solution.py:593
  45.0 0.0 copy-done.1
  45.1 0.0 copy-done
  45.1 0.0 copy-done.2
  45.1 1.6 %shard_map.104 = (f32[8,2048]{1,0:T(8,128)}, f32[8,8]{1,0:T(8,128)}, f32[8,8]{1,0:T(8,128)}) custom-call(f32[8,2048]{1,0:T(8,128)S(1)} %get-tuple-element.6.shifted, f32[16,128]{1,0:T(8,128)S(1)} %get-tuple-element.7.early, f32[2,128]{1,0:T(2,128)S(1)} %get-tuple-element.8.final, f32[8,2048]{1,0:T(8,128)S(1)} %copy-done, f32[8,2048]{1,0:T(8,128)S(1)} %copy-done.1, ...), custom_call_target="tpu_custom_call" | custom-call | tf_op jit(solution)/shard_map/pallas_call | solution.py:664
Async XLA Ops:
  0.6 44.4 %copy-start.1 = (f32[8,2048]{1,0:T(8,128)S(1)}, f32[8,2048]{1,0:T(8,128)}, u32[]{:S(2)}) copy-start(f32[8,2048]{1,0:T(8,128)} %prev.1) | copy-start | bytes 196612
  0.6 44.4 %copy-start = (f32[8,2048]{1,0:T(8,128)S(1)}, f32[8,2048]{1,0:T(8,128)}, u32[]{:S(2)}) copy-start(f32[8,2048]{1,0:T(8,128)} %now.1) | copy-start | bytes 196612
  0.7 44.4 %copy-start.2 = (f32[8,8]{1,0:T(8,128)S(1)}, f32[8,8]{1,0:T(8,128)}, u32[]{:S(2)}) copy-start(f32[8,8]{1,0:T(8,128)} %coupling.1) | copy-start | bytes 772

commit v6 on v5

--- a/solution.py
+++ b/solution.py
@@ -335,7 +335,7 @@
     phase("split2")
     split_vectors(row_vec, row_split)
     phase("prodcols1")
-    products(0, UNROLL, rows_s, row_split, False)
+    products(0, 2 * UNROLL, rows_s, row_split, False)
     phase("waitpair")
     arrived(row_pair, pair_sem.at[0], (r, pair))
     mine = half_of(core)
@@ -352,7 +352,9 @@
     for peer in row_group:
         send(early_send.at[0], early_one.at[c], one_sem.at[c], peer)
     phase("prodcols2")
-    products(UNROLL, 3 * UNROLL, rows_s, row_split, False)
+    products(2 * UNROLL, 3 * UNROLL, rows_s, row_split, False)
+    phase("prodcols3")
+    products(3 * UNROLL, slots, rows_s, row_split, False)
     phase("rowfar")
     opposite = xs[0] * 2 * count
     for d, (yy, peer) in enumerate([(1 - yhi, across), (yhi, (r, col_of(yhi, xs[0], core)))]):
@@ -362,8 +364,6 @@
             ring_sem.at[2 + d],
             peer,
         )
-    phase("prodcols3")
-    products(3 * UNROLL, slots, rows_s, row_split, False)
     phase("scatcols")
     scatter(cols_v[...], part_cols)
 

time: 46.9 us -> 46.7 us (level)
  no operation moved by 1% of the time
where the time goes in v6:
time: 46.7 us; the launch traced here: 46.5 us
  Pallas kernels  45.1 us (97%)
  between operations  1.37 us (3%)
    pallas_call x1, Pallas kernels, local(): pl.pallas_call(kernel, out_shape=(shape((vectors, width), F32), shape((16...  43.5 us
    pallas_call x1, Pallas kernels, local(): pl.pallas_call(functools.partial(finish, 1.0 / (width * n_row * n_col)),...  1.63 us

profile of v6, /device:TPU:1, one launch (start us, length us, event | category | flops | bytes accessed | tf_op | source)
XLA Modules:
  0.0 46.5 jit_solution(13040140433951261321)
XLA Ops:
  0.6 0.0 copy-start.1
  0.6 0.0 copy-start
  0.7 0.0 copy-start.2
  1.3 43.5 %shard_map.103 = (f32[8,2048]{1,0:T(8,128)S(1)}, f32[16,128]{1,0:T(8,128)S(1)}, f32[2,128]{1,0:T(2,128)S(1)}) custom-call(f32[256,128,128]{2,1,0:T(8,128)} %bitcast.6, s32[256]{0:T(256)} %bitcast.8, s32[256]{0:T(256)} %bitcast.10, s32[1,1]{1,0:T(1,128)S(6)} %copy.11.count_h, s32[1,256]{1,0:T(1,128)} %bitcast.9, s32[1,256]{1,0:T(1,128)} %bitcast.11, ...), custom_call_target="tpu_custom_call" | custom-call | tf_op jit(solution)/shard_map/pallas_call | solution.py:593
  44.8 0.0 copy-done.1
  44.8 0.0 copy-done
  44.9 0.0 copy-done.2
  44.9 1.6 %shard_map.104 = (f32[8,2048]{1,0:T(8,128)}, f32[8,8]{1,0:T(8,128)}, f32[8,8]{1,0:T(8,128)}) custom-call(f32[8,2048]{1,0:T(8,128)S(1)} %get-tuple-element.6.shifted, f32[16,128]{1,0:T(8,128)S(1)} %get-tuple-element.7.early, f32[2,128]{1,0:T(2,128)S(1)} %get-tuple-element.8.final, f32[8,2048]{1,0:T(8,128)S(1)} %copy-done, f32[8,2048]{1,0:T(8,128)S(1)} %copy-done.1, ...), custom_call_target="tpu_custom_call" | custom-call | tf_op jit(solution)/shard_map/pallas_call | solution.py:664
Async XLA Ops:
  0.6 44.2 %copy-start.1 = (f32[8,2048]{1,0:T(8,128)S(1)}, f32[8,2048]{1,0:T(8,128)}, u32[]{:S(2)}) copy-start(f32[8,2048]{1,0:T(8,128)} %prev.1) | copy-start | bytes 196612
  0.6 44.2 %copy-start = (f32[8,2048]{1,0:T(8,128)S(1)}, f32[8,2048]{1,0:T(8,128)}, u32[]{:S(2)}) copy-start(f32[8,2048]{1,0:T(8,128)} %now.1) | copy-start | bytes 196612
  0.7 44.2 %copy-start.2 = (f32[8,8]{1,0:T(8,128)S(1)}, f32[8,8]{1,0:T(8,128)}, u32[]{:S(2)}) copy-start(f32[8,8]{1,0:T(8,128)} %coupling.1) | copy-start | bytes 772
